TPU v7x, 256 devices: a whole 4x4x8 slice. The times are simulated.
256 devices in a mesh: depth: 128 (over y, x, z_lo, core), src: 2 (over z_hi).
Axes of the slice: x: 4, y: 4, z: 8 (z_hi: 2, z_lo: 4; z = z_hi * 4 + z_lo), core: 2. Of those that a mesh axis runs over, the one named last changes fastest.
Arguments:
- angles: int32 [4], P('src'), may hold values from 0 to 63
- factor_choice: int32 [256], P('depth'), may hold values from 0 to 1
- contrast: float32 [256, 256], P('depth'), may hold values from -1 to 1
- adjoint_source: float32 [2, 4, 256, 256], P(None, 'src', 'depth'), may hold values from -1 to 1
- inverse_blocks: float32 [256, 2, 2, 128, 128], P('depth')
Outputs:
- gradient: float32 [256, 256], P('depth', 'src')
All inputs are finite; a program needn't handle non-finite values.
Results may differ from a plain program's by a relative error of at most 0.0003.
Values sent between devices are 32-bit elements; how exact they have to be, the bound alone decides.
No kernel may reach another device: no remote copies, remote signals or barrier semaphores. Data moves between devices by JAX's collectives and lax.ppermute only.
A program may use at most 192 MiB of HBM per device.

v0:
```python
import math

import jax
import jax.numpy as jnp
from jax import lax
from jax.sharding import PartitionSpec as P

B = 128
NANG = 64


PRECISE = lax.Precision.HIGHEST
WAVENUMBER = 0.8


def prefix(value, axis, combine, identity, reverse):
    length, place = (lax.axis_size(axis), lax.axis_index(axis))
    everything = jax.tree.map(lambda part: lax.all_gather(part, axis), value)
    start = jax.tree.map(
        lambda part, zero: jnp.broadcast_to(jnp.asarray(zero, part.dtype), part.shape),
        value,
        identity,
    )

    def step(k, before):
        at = length - 1 - k if reverse else k
        reached = at > place if reverse else at < place
        new = combine(before, jax.tree.map(lambda part: part[at], everything))
        return jax.tree.map(lambda a, b: jnp.where(reached, a, b), new, before)

    return lax.fori_loop(0, length, step, start)


def apply_block(factor, carried):
    real_part = jnp.einsum(
        "tij,ftj->fti", factor[:, 0], carried[0], precision=PRECISE
    ) - jnp.einsum("tij,ftj->fti", factor[:, 1], carried[1], precision=PRECISE)
    imag_part = jnp.einsum(
        "tij,ftj->fti", factor[:, 0], carried[1], precision=PRECISE
    ) + jnp.einsum("tij,ftj->fti", factor[:, 1], carried[0], precision=PRECISE)
    return jnp.stack([real_part, imag_part])


def compose(later, earlier):
    real_part = jnp.einsum(
        "tij,tjk->tik", later[:, 0], earlier[:, 0], precision=PRECISE
    ) - jnp.einsum("tij,tjk->tik", later[:, 1], earlier[:, 1], precision=PRECISE)
    imag_part = jnp.einsum(
        "tij,tjk->tik", later[:, 0], earlier[:, 1], precision=PRECISE
    ) + jnp.einsum("tij,tjk->tik", later[:, 1], earlier[:, 0], precision=PRECISE)
    return jnp.stack([real_part, imag_part], axis=1)


def combine(earlier, later):
    return (compose(later[0], earlier[0]), apply_block(later[0], earlier[1]) + later[1])


def identity_pair(tile_count, width, fields):
    unit = jnp.stack([jnp.eye(width, dtype=jnp.float32), jnp.zeros((width, width), jnp.float32)])
    unit = jnp.broadcast_to(unit[None], (tile_count, 2, width, width))
    return (unit, jnp.zeros((2, fields, tile_count, width), jnp.float32))


def incident_wave(angles, layers, first_layer, lateral_cells):
    direction = angles.astype(jnp.float32) * (2.0 * math.pi / NANG)
    depth_pos = first_layer + jnp.arange(layers).astype(jnp.float32)
    lateral = (jnp.arange(lateral_cells) % B).astype(jnp.float32)
    phase_arg = WAVENUMBER * (
        jnp.sin(direction)[:, None, None] * lateral[None, None, :]
        + jnp.cos(direction)[:, None, None] * depth_pos[None, :, None]
    )
    return jnp.stack([jnp.cos(phase_arg), jnp.sin(phase_arg)])


def boundary_values(mapping, offset, backward):
    tile_count = mapping.shape[0]
    width = mapping.shape[2]
    result = prefix(
        (mapping, offset),
        "depth",
        combine,
        identity_pair(tile_count, width, offset.shape[1]),
        backward,
    )
    return result[1]


def per_device(angles, factor_choice, contrast, adjoint_source, inverse_blocks):
    sources = angles.shape[0]
    layers, lateral_cells = contrast.shape
    width = inverse_blocks.shape[3]
    tile_count = lateral_cells // width
    first_layer = (lax.axis_index("depth") * layers).astype(jnp.float32)
    incident = incident_wave(angles, layers, first_layer, lateral_cells)
    forcing = incident * contrast[None, None]
    fields = jnp.concatenate([forcing, adjoint_source], axis=1)
    fields = fields.reshape(2, 2 * sources, layers, tile_count, width).transpose(2, 0, 1, 3, 4)
    factors = [
        lax.dynamic_index_in_dim(inverse_blocks, factor_choice[level], 0, keepdims=False)
        for level in range(layers)
    ]
    zero_state = jnp.zeros(fields.shape[1:], jnp.float32)

    def sweep_down(incoming):
        carried = incoming
        results = []
        for level in range(layers):
            carried = apply_block(factors[level], fields[level] + carried)
            results.append(carried)
        return results

    def sweep_up(downward, incoming):
        carried = incoming
        results = [None] * layers
        for level in range(layers - 1, -1, -1):
            carried = downward[level] + apply_block(factors[level], carried)
            results[level] = carried
        return results

    down_map = factors[0]
    level = 1
    down_map = compose(factors[level], down_map)
    local_down = sweep_down(zero_state)[-1]
    incoming_down = boundary_values(down_map, local_down, False)
    downward = sweep_down(incoming_down)
    up_map = factors[layers - 1]
    level = 0
    up_map = compose(factors[level], up_map)
    local_up = sweep_up(downward, zero_state)[0]
    incoming_up = boundary_values(up_map, local_up, True)
    upward = sweep_up(downward, incoming_up)
    solved = (
        jnp.stack(upward).transpose(1, 2, 0, 3, 4).reshape(2, 2 * sources, layers, lateral_cells)
    )
    total_field = incident + solved[:, :sources]
    adjoint = solved[:, sources:]
    all_sources = sources * lax.axis_size("src")
    terms = jnp.sum(total_field[0] * adjoint[0] - total_field[1] * adjoint[1], axis=0) / all_sources
    return lax.psum_scatter(terms, "src", scatter_dimension=1, tiled=True)


def solution(mesh):
    placed = (
        P("src"),
        P("depth"),
        P("depth", None),
        P(None, "src", "depth", None),
        P("depth", None, None, None, None),
    )
    return jax.shard_map(
        per_device, mesh=mesh, in_specs=placed, out_specs=P("depth", "src"), check_vma=False
    )
```

profile of v0, /device:TPU:1, one launch (start us, length us, event | category | flops | bytes accessed | tf_op | source)
XLA Modules:
  0.0 1455.1 jit_solution(15672423084577046918)
XLA Ops:
  6.5 1.3 fusion.62
  13.9 1.1 constant_dynamic-slice_fusion
  22.7 197.1 %all-gather.12.cloned.1.call-done = f32[256,4,2,128]{3,1,2,0:T(4,128)} async-done(((f32[2,4,2,128]{3,1,2,0:T(4,128)}), f32[256,4,2,128]{3,1,2,0:T(4,128)}) %all-gather.12.cloned.1.call-update) | async-done | bytes 1048592 | tf_op jit(solution)/shard_map/all_gather | solution.py:18
  219.8 236.3 %all-gather.10.cloned.1.call-done = f32[256,2,128,128]{3,2,0,1:T(8,128)} async-done(((f32[2,2,128,128]{3,2,0,1:T(8,128)}), f32[256,2,128,128]{3,2,0,1:T(8,128)}) %all-gather.10.cloned.1.call-update) | async-done | bytes 33554448 | tf_op jit(solution)/shard_map/all_gather | solution.py:18
  456.1 383.6 %while.30 = (s32[]{:T(128)}, f32[2,4,2,128]{3,1,2,0:T(4,128)S(1)}, s32[]{:T(128)}, f32[128,2,2,128,128]{4,3,1,0,2:T(8,128)}, f32[128,2,4,2,128]{4,2,3,1,0:T(4,128)}, /*index=5*/s32[]{:T(128)}, s32[]{:T(128)}) while((s32[]{:T(128)}, f32[2,4,2,128]{3,1,2,0:T(4,128)S(1)}, s32[]{:T(128)}, f32[128,2,2,128,128]{4,3,1,0,2:T(8,128)}, ...), condition=%wide.region_1.2_spmd.clone, body=%wide.region_0.1_spmd.clone.sunk | while | flops 6303748 | bytes 1138794 | solution.py:31
  471.1 1.0 dynamic-slice_bitcast_fusion.4
  474.1 1.0 dynamic-slice_bitcast_fusion.4
  480.1 1.0 dynamic-slice_bitcast_fusion.4
  486.1 1.0 dynamic-slice_bitcast_fusion.4
  492.1 1.0 dynamic-slice_bitcast_fusion.4
  498.1 1.0 dynamic-slice_bitcast_fusion.4
  510.1 1.0 dynamic-slice_bitcast_fusion.4
  513.1 1.0 dynamic-slice_bitcast_fusion.4
  519.1 1.0 dynamic-slice_bitcast_fusion.4
  522.1 1.0 dynamic-slice_bitcast_fusion.4
  525.1 1.0 dynamic-slice_bitcast_fusion.4
  528.1 1.0 dynamic-slice_bitcast_fusion.4
  531.1 1.0 dynamic-slice_bitcast_fusion.4
  534.1 1.0 dynamic-slice_bitcast_fusion.4
  540.1 1.0 dynamic-slice_bitcast_fusion.4
  543.1 1.0 dynamic-slice_bitcast_fusion.4
  552.1 1.0 dynamic-slice_bitcast_fusion.4
  555.1 1.0 dynamic-slice_bitcast_fusion.4
  558.1 1.0 dynamic-slice_bitcast_fusion.4
  561.1 1.0 dynamic-slice_bitcast_fusion.4
  564.1 1.0 dynamic-slice_bitcast_fusion.4
  576.1 1.0 dynamic-slice_bitcast_fusion.4
  582.1 1.0 dynamic-slice_bitcast_fusion.4
  588.1 1.0 dynamic-slice_bitcast_fusion.4
  591.1 1.0 dynamic-slice_bitcast_fusion.4
  594.1 1.0 dynamic-slice_bitcast_fusion.4
  597.2 1.0 dynamic-slice_bitcast_fusion.4
  600.2 1.0 dynamic-slice_bitcast_fusion.4
  606.2 1.0 dynamic-slice_bitcast_fusion.4
  609.1 1.0 dynamic-slice_bitcast_fusion.4
  612.1 1.0 dynamic-slice_bitcast_fusion.4
  624.2 1.0 dynamic-slice_bitcast_fusion.4
  627.2 1.0 dynamic-slice_bitcast_fusion.4
  630.2 1.0 dynamic-slice_bitcast_fusion.4
  633.1 1.0 dynamic-slice_bitcast_fusion.4
  636.2 1.0 dynamic-slice_bitcast_fusion.4
  642.2 1.0 dynamic-slice_bitcast_fusion.4
  645.2 1.0 dynamic-slice_bitcast_fusion.4
  648.2 1.0 dynamic-slice_bitcast_fusion.4
  844.4 196.0 %all-gather.8.cloned.1.call-done = f32[128,2,4,2,128]{4,2,3,1,0:T(4,128)} async-done(((f32[1,2,4,2,128]{4,2,3,1,0:T(4,128)}), f32[128,2,4,2,128]{4,2,3,1,0:T(4,128)}) %all-gather.8.cloned.1.call-update) | async-done | bytes 1048592 | tf_op jit(solution)/shard_map/all_gather | solution.py:18
  1040.4 383.9 %while.31 = (s32[]{:T(128)}, f32[2,4,2,128]{3,1,2,0:T(4,128)S(1)}, s32[]{:T(128)}, f32[128,2,2,128,128]{4,3,1,0,2:T(8,128)}, f32[128,2,4,2,128]{4,2,3,1,0:T(4,12...) while((s32[]{:T(128)}, f32[2,4,2,128]{3,1,2,0:T(4,128)S(1)}, s32[]{:T(128)}, ...), condition=%wide.region_3.4_spmd.clone, body=%wide.region_2.3_spmd.clone.sunk | while | flops 6303752 | bytes 1138856 | solution.py:31
  1427.8 19.3 %reduce-scatter.4.cloned.1.call-done = f32[128,2]{1,0:T(8,128)} async-done(((f32[256,2]{1,0:T(8,128)}), f32[128,2]{1,0:T(8,128)}) %reduce-scatter.4.cloned.1.call-update) | async-done | bytes 1040
  1447.1 1.5 copy.23
  (1832 shorter events, 744.1 us)
Async XLA Ops:
  6.5 213.3 %all-gather.12.cloned.1.call-start = ((), (), s32[]{:S(2)}) async-start(), calls=%async_computation.3 | async-start | bytes 1056768 | tf_op jit(solution)/shard_map/all_gather | solution.py:18
  18.2 438.0 %all-gather.10.cloned.1.call-start = ((), (), s32[]{:S(2)}) async-start(), calls=%async_computation.2 | async-start | bytes 33816576 | tf_op jit(solution)/shard_map/all_gather | solution.py:18
  20.1 824.3 %all-gather.14.cloned.1.call-start = ((), (), s32[]{:S(2)}) async-start(), calls=%async_computation.4 | async-start | bytes 33816576 | tf_op jit(solution)/shard_map/all_gather | solution.py:18
  22.0 1018.4 %all-gather.8.cloned.1.call-start = ((), (), s32[]{:S(2)}) async-start(), calls=%async_computation.1 | async-start | bytes 1056768 | tf_op jit(solution)/shard_map/all_gather | solution.py:18
  844.3 602.8 %reduce-scatter.4.cloned.1.call-start = ((), (), s32[]{:S(2)}) async-start(), calls=%async_computation.5 | async-start | bytes 196608
Sparse Core Ops, SparseCore 0:
  18.3 201.4 all-gather.11
  221.7 234.3 all-gather.9
  458.0 235.1 all-gather.13
  844.4 195.8 all-gather.7
  1427.9 19.1 reduce-scatter.3
where the time goes:
time: 1470 us; the launch traced here: 1460 us
  waiting for transfers between devices  649 us (44%)
  matrix products  339 us (23%)
  local copies, waits for them, and re-layouts  253 us (17%)
  other arithmetic  194 us (13%)
  between operations  17 us (1%)
    all_gather x4, waiting for transfers between devices, prefix(): everything = jax.tree.map(lambda part: lax.all_gather(part, axis), value)  629 us
    squeeze x256, local copies, waits for them, and re-layouts, step(): new = combine(before, jax.tree.map(lambda part: part[at], everything))  249 us
    select_n x256, other arithmetic, step(): return jax.tree.map(lambda a, b: jnp.where(reached, a, b), new, before)  187 us
    dot_general x264, matrix products, apply_block(): jnp.einsum('tij,ftj->fti', factor[:, 1], carried[1], precision=PRECISE)  85.7 us
    dot_general x263, matrix products, apply_block(): jnp.einsum('tij,ftj->fti', factor[:, 1], carried[0], precision=PRECISE)  85.4 us
    dot_general x263, matrix products, apply_block(): jnp.einsum('tij,ftj->fti', factor[:, 0], carried[1], precision=PRECISE)  85 us
    dot_general x264, matrix products, apply_block(): jnp.einsum('tij,ftj->fti', factor[:, 0], carried[0], precision=PRECISE)  80.6 us
  transfers between devices with their start and end apart: 5, of which 4 were waited for; matrix products, arithmetic and copies ran while one was open for 27% of the time, Pallas kernels for 0%

commit v1 on v0

v1 whole, which is shorter than its diff:
```python
import functools
import math

import jax
import jax.numpy as jnp
from jax import lax
from jax.experimental import pallas as pl
from jax.experimental.pallas import tpu as pltpu
from jax.sharding import PartitionSpec as P

B = 128
W2 = 2 * B
NANG = 64
WAVENUMBER = 0.8
FIELDS = 8
ROWS = B + FIELDS
F32 = jnp.float32
BF16 = jnp.bfloat16


def split(v):
    hi = v.astype(BF16)
    return hi, (v - hi.astype(F32)).astype(BF16)


def wide(part):
    re, im = part[:, :B], part[:, B:]
    return jnp.concatenate([part, jnp.concatenate([-im, re], axis=1)], axis=0)


def weights(t):
    hi, lo = split(t)
    return wide(hi), wide(lo)


def dot(a, b):
    return jnp.dot(a, b, preferred_element_type=F32)


def mul(v, w):
    hi, lo = split(v)
    return (dot(lo, w[0]) + dot(hi, w[1])) + dot(hi, w[0])


def mulv(v, w):
    n = v.shape[0]
    hi, lo = split(v)
    both = jnp.concatenate([hi, lo], axis=0)
    a, b = dot(both, w[0]), dot(both, w[1])
    return (a[n:] + b[:n]) + a[:n]


def coords():
    d = lax.axis_index("depth")
    return d & 1, (d >> 1) & 3, (d >> 3) & 3, (d >> 5) & 3


def place(shift):
    d = lax.axis_index("depth")
    core = d & 1
    at = (d >> shift) & 3
    return jnp.where(core == 0, at, 3 - at)


def prep_kernel(angles, choice, contrast, adj, blocks, own, oth, raw, sem):
    t = lax.axis_index("src")
    first = (lax.axis_index("depth") * 2).astype(F32)
    copies = [
        pltpu.make_async_copy(blocks.at[choice[l], t], raw.at[l], sem.at[l]) for l in range(2)
    ]
    for c in copies:
        c.start()
    row = lax.broadcasted_iota(jnp.int32, (FIELDS, B), 0)
    lane = lax.broadcasted_iota(jnp.int32, (FIELDS, B), 1).astype(F32)
    odd = (row & 1) == 1
    unit = 2.0 * math.pi / NANG
    direction = (
        jnp.where(odd, jnp.full((FIELDS, B), angles[1]), jnp.full((FIELDS, B), angles[0])).astype(F32)
        * unit
    )
    sn, cs = jnp.sin(direction), jnp.cos(direction)
    zero = jnp.zeros((FIELDS, B), F32)
    for l in range(2):
        arg = WAVENUMBER * (sn * lane + cs * (first + float(l)))
        inc = (jnp.cos(arg), jnp.sin(arg))
        for out, tile, shift, top in ((own, t, 0, B), (oth, 1 - t, 2, 0)):
            is_f = (row >= shift) & (row < shift + 2)
            is_a = (row >= shift + 4) & (row < shift + 6)

            def tiled(line):
                return jnp.where(tile == 0, line[:, :B], line[:, B:])

            con = tiled(contrast[pl.ds(l, 1), :])
            for p in range(2):
                a = jnp.where(odd, tiled(adj[p, 1, pl.ds(l, 1), :]), tiled(adj[p, 0, pl.ds(l, 1), :]))
                part = slice(p * B, (p + 1) * B)
                out[l, top : top + 8, part] = jnp.where(is_f, inc[p] * con, jnp.where(is_a, a, zero))
                out[l, top + 8 : top + 16, part] = jnp.where(is_f, inc[p], zero)
    for l in range(2):
        copies[l].wait()
        own[l, :B, :B] = raw[l, 0].T
        own[l, :B, B:] = raw[l, 1].T


def chip_kernel(own, peer, x):
    core = lax.axis_index("depth") & 1
    g = [(own if s < 2 else peer)[(s & 1) ^ core, :B, :] for s in range(4)]
    x01 = mul(g[0], weights(g[1]))
    x23 = mul(g[2], weights(g[3]))
    x[...] = mul(x01, weights(x23))


def offset_kernel(own, peer, same, cross, xm, x):
    core = lax.axis_index("depth") & 1
    x[:B, :] = xm[...]
    v = jnp.zeros((FIELDS, W2), F32)
    for k in range(4):
        a, b = (own, same) if k < 2 else (peer, cross)
        h = a[k & 1, B : B + 8, :] + b[k & 1, :8, :]
        v = mulv(v + h, weights(a[k & 1, :B, :]))
    x[B:, :] = jnp.where(core == 0, v, 0.0)


def level_kernel(shift, r0, r1, r2, r3, x, s, p, v):
    q = place(shift)
    for k, r in enumerate((r0, r1, r2, r3)):
        s[q ^ k] = r[...]
    row = lax.broadcasted_iota(jnp.int32, (ROWS, W2), 0)
    col = lax.broadcasted_iota(jnp.int32, (ROWS, W2), 1)
    tail = row >= B

    def step(a, b):
        return mul(a, weights(b[:B])) + jnp.where(tail, b, 0.0)

    s0, s1, s2, s3 = (s[k] for k in range(4))
    x01 = step(s0, s1)
    x23 = step(s2, s3)
    x[...] = step(x01, x23)
    x012 = step(x01, s2)
    one = jnp.where((row == col) & (row < B), 1.0, 0.0)
    p[...] = jnp.where(q == 0, one, jnp.where(q == 1, s0, jnp.where(q == 2, x01, x012)))
    v[0] = x23[:B]
    v[1] = mul(s1[:B], weights(x23[:B]))


def turn_kernel(r0, r1, r2, r3, pz, px, own, peer, same, cross, out, s):
    q = place(5)
    for k, r in enumerate((r0, r1, r2, r3)):
        s[q ^ k] = r[...]
    a = jnp.where(q > 0, s[0, B:, :], 0.0)
    for k in (1, 2):
        a = jnp.where(q > k, mulv(a, weights(s[k, :B, :])) + s[k, B:, :], a)
    for p in (px, pz):
        a = mulv(a, weights(p[:B, :])) + p[B:, :]
    ws, ds = [], []
    for k in range(4):
        g, o = (own, same) if k < 2 else (peer, cross)
        w = weights(g[k & 1, :B, :])
        a = mulv(a + (g[k & 1, B : B + 8, :] + o[k & 1, :8, :]), w)
        ws.append(w)
        ds.append(a)
        out[8 + 8 * k : 16 + 8 * k, :] = a
    u = ds[3]
    for k in (2, 1, 0):
        u = ds[k] + mulv(u, ws[k])
    out[:8, :] = u


def gather_kernel(shift, r0, r1, r2, r3, s, v, total, part, e):
    q = place(shift)
    for k, r in enumerate((r0, r1, r2, r3)):
        e[q ^ k] = r[...]
    total[...] = (
        (mulv(e[0], weights(v[1])) + mulv(e[1], weights(v[0])))
        + mulv(e[2], weights(s[3, :B, :]))
        + e[3]
    )
    c = jnp.where(q > 0, e[0], 0.0)
    for k in (1, 2):
        c = jnp.where(q > k, mulv(c, weights(s[k, :B, :])) + e[k], c)
    part[...] = c


def last_kernel(e0, e1, e2, e3, r0, r1, r2, r3, px, pz, cx, cz, own, peer, same, cross, d, grad, e, s):
    q = place(5)
    for k, (f, r) in enumerate(((e0, r0), (e1, r1), (e2, r2), (e3, r3))):
        e[q ^ k] = f[...]
        s[q ^ k] = r[...]
    u = jnp.where(q > 0, e[0], 0.0)
    for k in (1, 2):
        u = jnp.where(q > k, mulv(u, weights(s[k, :B, :])) + e[k], u)
    for p, c in ((px, cx), (pz, cz)):
        u = mulv(u, weights(p[:B, :])) + c[...]
    for k in (3, 2, 1, 0):
        g, o = (peer, cross) if k < 2 else (own, same)
        u = d[8 + 8 * k : 16 + 8 * k, :] + mulv(u, weights(g[k & 1, :B, :]))
        f = u + (g[k & 1, B + 8 : B + 16, :] + o[k & 1, 8:16, :])
        prod = f[:4] * f[4:]
        tot = jnp.sum(prod, axis=0, keepdims=True)
        grad[k : k + 1, :] = (tot[:, :B] - tot[:, B:]) * 0.25


def call(kernel, outs, *args, scratch=(), in_specs=None, name=None):
    shapes = [jax.ShapeDtypeStruct(o, F32) for o in outs]
    vm = pl.BlockSpec(memory_space=pltpu.VMEM)
    got = pl.pallas_call(
        kernel,
        out_shape=shapes,
        in_specs=in_specs or [vm] * len(args),
        out_specs=[vm] * len(outs),
        scratch_shapes=list(scratch),
        cost_estimate=pl.CostEstimate(flops=200_000_000, bytes_accessed=1_000_000, transcendentals=0),
        name=name,
    )(*args)
    return got[0] if len(outs) == 1 else got


def gather4(value, bit, depth, odd_only=False):
    pick = [i for i in range(depth) if not odd_only or i & 1]
    return [value] + [
        lax.ppermute(value, "depth", [(i, i ^ (k * bit)) for i in pick]) for k in (1, 2, 3)
    ]


def per_device(angles, factor_choice, contrast, adjoint_source, inverse_blocks):
    depth = lax.axis_size("depth")
    core = lax.axis_index("depth") & 1
    vm = pl.BlockSpec(memory_space=pltpu.VMEM)
    sm = pl.BlockSpec(memory_space=pltpu.SMEM)
    own, oth = call(
        prep_kernel,
        [(2, B + 16, W2), (2, 16, W2)],
        angles, factor_choice, contrast, adjoint_source, inverse_blocks,
        in_specs=[sm, sm, vm, vm, pl.BlockSpec(memory_space=pl.ANY)],
        scratch=[pltpu.VMEM((2, 2, B, B), F32), pltpu.SemaphoreType.DMA((2,))],
        name="prep",
    )
    swap = [(i, i ^ 1) for i in range(depth)]
    peer = lax.ppermute(own, "depth", swap)
    same = lax.ppermute(oth, "src", [(0, 1), (1, 0)])
    cross = lax.ppermute(
        oth, ("depth", "src"), [(2 * i + t, 2 * (i ^ 1) + (1 - t)) for i in range(depth) for t in range(2)]
    )
    xm = call(chip_kernel, [(B, W2)], own, peer, name="chip")
    x = call(offset_kernel, [(ROWS, W2)], own, peer, same, cross, xm, name="offset")
    outs = [(ROWS, W2), (4, ROWS, W2), (ROWS, W2), (2, B, W2)]
    x, sz, pz, vz = call(functools.partial(level_kernel, 1), outs, *gather4(x, 2, depth), name="level_z")
    x, sx, px, vx = call(functools.partial(level_kernel, 3), outs, *gather4(x, 8, depth), name="level_x")
    ry = gather4(x, 32, depth)
    big = pltpu.VMEM((4, ROWS, W2), F32)
    small = pltpu.VMEM((4, FIELDS, W2), F32)
    sent = call(
        turn_kernel, [(40, W2)], *ry, pz, px, own, peer, same, cross, scratch=[big], name="turn"
    )
    d = lax.ppermute(sent, "depth", [(i, i + 1) for i in range(0, depth, 2)])
    two = [(FIELDS, W2), (FIELDS, W2)]
    ez = gather4(d[:FIELDS], 2, depth, True)
    e, cz = call(functools.partial(gather_kernel, 1), two, *ez, sz, vz, scratch=[small], name="up_z")
    ex = gather4(e, 8, depth, True)
    e, cx = call(functools.partial(gather_kernel, 3), two, *ex, sx, vx, scratch=[small], name="up_x")
    ey = gather4(e, 32, depth, True)
    grad = call(
        last_kernel, [(4, B)], *ey, *ry, px, pz, cx, cz, own, peer, same, cross, d,
        scratch=[small, big], name="last",
    )
    back = lax.ppermute(grad[:2], "depth", [(i + 1, i) for i in range(0, depth, 2)])
    return jnp.where(core == 0, back, grad[2:])


def solution(mesh):
    placed = (
        P("src"),
        P("depth"),
        P("depth", None),
        P(None, "src", "depth", None),
        P("depth", None, None, None, None),
    )
    return jax.shard_map(
        per_device, mesh=mesh, in_specs=placed, out_specs=P("depth", "src"), check_vma=False
    )
```

time: 1470 us -> 121 us (0.08)
  waiting for transfers between devices: 649 us -> 38.7 us
  matrix products: 339 us -> 0 us
  local copies, waits for them, and re-layouts: 253 us -> 5.82 us
  other arithmetic: 194 us -> 0.57 us
  starting transfers between devices: 0.17 us -> 52.4 us
  Pallas kernels: 0 us -> 23 us
  between operations: 17 us -> 0.25 us
    all_gather x4 -> x0, waiting for transfers between devices: 629 us -> none  [prefix(): everything = jax.tree.map(lambda part: lax.all_gather(part, axis), value)]
    dot_general x1062 -> x0, matrix products: 339 us -> none  [the longest x264 85.7 us: apply_block(): jnp.einsum('tij,ftj->fti', factor[:, 1], carried[1], precision=PRECISE)]
    squeeze x257 -> x0, local copies, waits for them, and re-layouts: 249 us -> none  [the longest x256 249 us: step(): new = combine(before, jax.tree.map(lambda part: part[at], everything))]
    select_n x256 -> x1, other arithmetic: 187 us -> 0.57 us  [per_device(): return jnp.where(core == 0, back, grad[2:])]
    ppermute x0 -> x23, starting transfers between devices: none -> 52.4 us  [the longest x18 40.9 us: gather4(): lax.ppermute(value, 'depth', [(i, i ^ k * bit) for i in pick])]
    ppermute x0 -> x23, waiting for transfers between devices: none -> 38.7 us  [the longest x18 26.4 us: gather4(): lax.ppermute(value, 'depth', [(i, i ^ k * bit) for i in pick])]
    pallas_call x0 -> x9, Pallas kernels: none -> 23 us  [call(): pl.pallas_call(kernel, out_shape=shapes, in_specs=in_specs or [vm] * len(...]
    unnamed x6 -> x0, waiting for transfers between devices: 19.4 us -> none
  transfers between devices with their start and end apart: 5 -> 23, of which waited for: 4 -> 14; matrix products, arithmetic and copies ran while one was open for 27% -> 0% of each run, Pallas kernels for 0% -> 2%
where the time goes in v1:
time: 121 us
  starting transfers between devices  52.4 us (43%)
  waiting for transfers between devices  38.7 us (32%)
  Pallas kernels  23 us (19%)
  local copies, waits for them, and re-layouts  5.82 us (5%)
    ppermute x18, starting transfers between devices, gather4(): lax.ppermute(value, 'depth', [(i, i ^ k * bit) for i in pick])  40.9 us
    ppermute x18, waiting for transfers between devices, gather4(): lax.ppermute(value, 'depth', [(i, i ^ k * bit) for i in pick])  26.4 us
    pallas_call x9, Pallas kernels, call(): pl.pallas_call(kernel, out_shape=shapes, in_specs=in_specs or [vm] * len(...  23 us
    ppermute x1, waiting for transfers between devices, per_device(): d = lax.ppermute(sent, 'depth', [(i, i + 1) for i in range(0, depth, 2)])  7.42 us
    ppermute x1, starting transfers between devices, per_device(): same = lax.ppermute(oth, 'src', [(0, 1), (1, 0)])  5.2 us
    unnamed x48, local copies, waits for them, and re-layouts  5.15 us
    ppermute x1, waiting for transfers between devices, per_device(): lax.ppermute(oth, ('depth', 'src'), [(2 * i + t, 2 * (i ^ 1) + (1 - t)) f...  4.12 us
    ppermute x1, starting transfers between devices, per_device(): peer = lax.ppermute(own, 'depth', swap)  3.29 us
  transfers between devices with their start and end apart: 23, of which 14 were waited for; matrix products, arithmetic and copies ran while one was open for 0% of the time, Pallas kernels for 2%

profile of v1, /device:TPU:1, one launch (start us, length us, event | category | flops | bytes accessed | tf_op | source)
XLA Modules:
  0.0 120.7 jit_solution(16612008510245344598)
XLA Ops:
  0.0 2.6 %prep.1 = (f32[2,144,256]{2,1,0:T(8,128)}, f32[2,16,256]{2,1,0:T(8,128)}) custom-call(s32[2]{0:T(128)} %angles.1, s32[2]{0:T(128)} %choice.1, f32[2,256]{1,0:T(2,128)} %contrast.1, f32[2,2,2,256]{3,2,1,0:T(2,128)} %adj.1, f32[2,2,2,128,128]{4,3,2,1,0:T(8,128)} %blocks.1), custom_call_target="tpu_custom_call" | custom-call | flops 200000000 | bytes 1000000 | tf_op jit(solution)/shard_map/prep/pallas_call | solution.py:206
  2.6 3.3 %collective-permute-start = (f32[2,144,256]{2,1,0:T(8,128)}, f32[2,144,256]{2,1,0:T(8,128)S(1)}, u32[]{:S(2)}, u32[]{:S(2)}) collective-permute-start(f32[2,144,256]{2,1,0:T(8,128)} %get-tuple-element.19.own), channel_id=1, source_target_pairs={{0,2},{2,0},{4,6},{6,4},{8,10},{10,8},{12,14},{14,12},{16,18},{18,... | collective-permute-start | bytes 884744 | tf_op jit(solution)/shard_map/ppermute | solution.py:239
  5.9 5.2 %collective-permute-start.1 = (f32[2,16,256]{2,1,0:T(8,128)}, f32[2,16,256]{2,1,0:T(8,128)S(1)}, u32[]{:S(2)}, u32[]{:S(2)}) collective-permute-start(f32[2,16,256]{2,1,0:T(8,128)} %get-tuple-element.20), channel_id=1, source_target_pairs={{0,1},{1,0},{2,3},{3,2},{4,5},{5,4},{6,7},{7,6},{8,9},{9,8},{10,11... | collective-permute-start | bytes 98312 | tf_op jit(solution)/shard_map/ppermute | solution.py:240
  11.5 0.7 copy-done
  12.2 2.2 %chip.1.xm = f32[128,256]{1,0:T(8,128)} custom-call(f32[2,144,256]{2,1,0:T(8,128)} %get-tuple-element.19.own, f32[2,144,256]{2,1,0:T(8,128)} %copy-done), custom_call_target="tpu_custom_call" | custom-call | flops 200000000 | bytes 1000000 | tf_op jit(solution)/shard_map/chip/pallas_call | solution.py:206
  14.5 4.1 %collective-permute-done.2.cross = f32[2,16,256]{2,1,0:T(8,128)S(1)} collective-permute-done((f32[2,16,256]{2,1,0:T(8,128)}, f32[2,16,256]{2,1,0:T(8,128)S(1)}, u32[]{:S(2)}, u32[]{:S(2)}) %collective-permute-start.2) | collective-permute-done | bytes 32800 | tf_op jit(solution)/shard_map/ppermute | solution.py:241
  18.6 0.6 copy-done.5
  19.2 2.3 %offset.1.r0 = f32[136,256]{1,0:T(8,128)} custom-call(f32[2,144,256]{2,1,0:T(8,128)} %get-tuple-element.19.own, f32[2,144,256]{2,1,0:T(8,128)} %copy-done, f32[2,16,256]{2,1,0:T(8,128)} %copy-done.4, f32[2,16,256]{2,1,0:T(8,128)} %copy-done.5, f32[128,256]{1,0:T(8,128)} %chip.1.xm), custom_call_target="tpu_custom_call" | custom-call | flops 200000000 | bytes 1000000 | tf_op jit(solution)/shard_map/offset/pallas_call | solution.py:206
  21.5 0.7 collective-permute-start.3
  22.2 1.5 %collective-permute-start.4 = (f32[136,256]{1,0:T(8,128)}, f32[136,256]{1,0:T(8,128)S(1)}, u32[]{:S(2)}, u32[]{:S(2)}) collective-permute-start(f32[136,256]{1,0:T(8,128)} %offset.1.r0), channel_id=1, source_target_pairs={{0,8},{2,10},{4,12},{6,14},{8,0},{10,2},{12,4},{14,6},{16,24},{18,... | collective-permute-start | bytes 417800 | tf_op jit(solution)/shard_map/ppermute | solution.py:221
  23.7 1.3 %collective-permute-start.5 = (f32[136,256]{1,0:T(8,128)}, f32[136,256]{1,0:T(8,128)S(1)}, u32[]{:S(2)}, u32[]{:S(2)}) collective-permute-start(f32[136,256]{1,0:T(8,128)} %offset.1.r0), channel_id=1, source_target_pairs={{0,12},{2,14},{4,8},{6,10},{8,4},{10,6},{12,0},{14,2},{16,28},{18,... | collective-permute-start | bytes 417800 | tf_op jit(solution)/shard_map/ppermute | solution.py:221
  25.0 3.3 %collective-permute-done.3.r1 = f32[136,256]{1,0:T(8,128)S(1)} collective-permute-done((f32[136,256]{1,0:T(8,128)}, f32[136,256]{1,0:T(8,128)S(1)}, u32[]{:S(2)}, u32[]{:S(2)}) %collective-permute-start.3) | collective-permute-done | bytes 139296 | tf_op jit(solution)/shard_map/ppermute | solution.py:221
  28.5 4.9 %collective-permute-done.5.r3 = f32[136,256]{1,0:T(8,128)S(1)} collective-permute-done((f32[136,256]{1,0:T(8,128)}, f32[136,256]{1,0:T(8,128)S(1)}, u32[]{:S(2)}, u32[]{:S(2)}) %collective-permute-start.5) | collective-permute-done | bytes 139296 | tf_op jit(solution)/shard_map/ppermute | solution.py:221
  33.5 0.7 copy-done.22
  34.1 2.5 %level_z.1 = (f32[136,256]{1,0:T(8,128)}, f32[4,136,256]{2,1,0:T(8,128)}, f32[136,256]{1,0:T(8,128)}, f32[2,128,256]{2,1,0:T(8,128)}) custom-call(f32[136,256]{1,0:T(8,128)} %offset.1.r0, f32[136,256]{1,0:T(8,128)} %copy-done.18, f32[136,256]{1,0:T(8,128)} %copy-done.20, f32[136,256]{1,0:T(8,128)} %copy-done.22), custom_call_target="tpu_custom_call" | custom-call | flops 200000000 | bytes 1000000 | tf_op jit(solution)/shard_map/level_z/pallas_call | solution.py:206
  36.6 1.2 %collective-permute-start.6 = (f32[136,256]{1,0:T(8,128)}, f32[136,256]{1,0:T(8,128)S(1)}, u32[]{:S(2)}, u32[]{:S(2)}) collective-permute-start(f32[136,256]{1,0:T(8,128)} %get-tuple-element.21.r0), channel_id=1, source_target_pairs={{0,16},{2,18},{4,20},{6,22},{8,24},{10,26},{12,28},{14,30},{16,0},... | collective-permute-start | bytes 417800 | tf_op jit(solution)/shard_map/ppermute | solution.py:221
  37.8 2.4 %collective-permute-start.7 = (f32[136,256]{1,0:T(8,128)}, f32[136,256]{1,0:T(8,128)S(1)}, u32[]{:S(2)}, u32[]{:S(2)}) collective-permute-start(f32[136,256]{1,0:T(8,128)} %get-tuple-element.21.r0), channel_id=1, source_target_pairs={{0,32},{2,34},{4,36},{6,38},{8,40},{10,42},{12,44},{14,46},{16,48}... | collective-permute-start | bytes 417800 | tf_op jit(solution)/shard_map/ppermute | solution.py:221
  40.7 3.7 %collective-permute-done.7.r2 = f32[136,256]{1,0:T(8,128)S(1)} collective-permute-done((f32[136,256]{1,0:T(8,128)}, f32[136,256]{1,0:T(8,128)S(1)}, u32[]{:S(2)}, u32[]{:S(2)}) %collective-permute-start.7) | collective-permute-done | bytes 139296 | tf_op jit(solution)/shard_map/ppermute | solution.py:221
  44.5 1.5 %collective-permute-done.8.r3 = f32[136,256]{1,0:T(8,128)S(1)} collective-permute-done((f32[136,256]{1,0:T(8,128)}, f32[136,256]{1,0:T(8,128)S(1)}, u32[]{:S(2)}, u32[]{:S(2)}) %collective-permute-start.8) | collective-permute-done | bytes 139296 | tf_op jit(solution)/shard_map/ppermute | solution.py:221
  45.9 0.7 copy-done.23
  46.6 2.5 %level_x.1 = (f32[136,256]{1,0:T(8,128)}, f32[4,136,256]{2,1,0:T(8,128)}, f32[136,256]{1,0:T(8,128)}, f32[2,128,256]{2,1,0:T(8,128)}) custom-call(f32[136,256]{1,0:T(8,128)} %get-tuple-element.21.r0, f32[136,256]{1,0:T(8,128)} %copy-done.19, f32[136,256]{1,0:T(8,128)} %copy-done.21, f32[136,256]{1,0:T(8,128)} %copy-done.23), custom_call_target="tpu_custom_call" | custom-call | flops 200000000 | bytes 1000000 | tf_op jit(solution)/shard_map/level_x/pallas_call | solution.py:206
  49.1 2.9 %collective-permute-start.10 = (f32[136,256]{1,0:T(8,128)}, f32[136,256]{1,0:T(8,128)S(1)}, u32[]{:S(2)}, u32[]{:S(2)}) collective-permute-start(f32[136,256]{1,0:T(8,128)} %get-tuple-element.22.r0), channel_id=1, source_target_pairs={{0,128},{2,130},{4,132},{6,134},{8,136},{10,138},{12,140},{14,142}... | collective-permute-start | bytes 417800 | tf_op jit(solution)/shard_map/ppermute | solution.py:221
  52.0 0.8 collective-permute-start.11
  52.8 1.9 %collective-permute-done.10.r2 = f32[136,256]{1,0:T(8,128)S(1)} collective-permute-done((f32[136,256]{1,0:T(8,128)}, f32[136,256]{1,0:T(8,128)S(1)}, u32[]{:S(2)}, u32[]{:S(2)}) %collective-permute-start.10) | collective-permute-done | bytes 139296 | tf_op jit(solution)/shard_map/ppermute | solution.py:221
  54.7 2.6 %collective-permute-done.11.r3 = f32[136,256]{1,0:T(8,128)S(1)} collective-permute-done((f32[136,256]{1,0:T(8,128)}, f32[136,256]{1,0:T(8,128)S(1)}, u32[]{:S(2)}, u32[]{:S(2)}) %collective-permute-start.11) | collective-permute-done | bytes 139296 | tf_op jit(solution)/shard_map/ppermute | solution.py:221
  57.3 0.6 copy-done.2
  58.0 3.4 %turn.1 = f32[40,256]{1,0:T(8,128)} custom-call(f32[136,256]{1,0:T(8,128)} %get-tuple-element.22.r0, f32[136,256]{1,0:T(8,128)} %copy-done.3, f32[136,256]{1,0:T(8,128)} %copy-done.1, f32[136,256]{1,0:T(8,128)} %copy-done.2, f32[136,256]{1,0:T(8,128)} %get-tuple-element.23.pz, f32[136,256]{1,0:T(8,128)} %get-tuple-element.24.px, ...), custom_call_target="tpu_custom_call" | custom-call | flops 200000000 | bytes 1000000 | tf_op jit(solution)/shard_map/turn/pallas_call | solution.py:206
  61.5 1.3 %collective-permute-start.12 = (f32[40,256]{1,0:T(8,128)}, f32[40,256]{1,0:T(8,128)S(1)}, u32[]{:S(2)}, u32[]{:S(2)}) collective-permute-start(f32[40,256]{1,0:T(8,128)} %turn.1), channel_id=1, source_target_pairs={{0,2},{4,6},{8,10},{12,14},{16,18},{20,22},{24,26},{28,30},{32,34}... | collective-permute-start | bytes 122888 | tf_op jit(solution)/shard_map/ppermute | solution.py:255
  62.8 7.4 %collective-permute-done.12.d = f32[40,256]{1,0:T(8,128)S(1)} collective-permute-done((f32[40,256]{1,0:T(8,128)}, f32[40,256]{1,0:T(8,128)S(1)}, u32[]{:S(2)}, u32[]{:S(2)}) %collective-permute-start.12) | collective-permute-done | bytes 40992 | tf_op jit(solution)/shard_map/ppermute | solution.py:255
  70.2 4.8 %collective-permute-start.13 = (f32[8,256]{1,0:T(8,128)S(1)}, f32[8,256]{1,0:T(8,128)S(1)}, u32[]{:S(2)}, u32[]{:S(2)}) collective-permute-start(f32[8,256]{1,0:T(8,128)S(1)} %slice.12.r0), channel_id=1, source_target_pairs={{2,6},{6,2},{10,14},{14,10},{18,22},{22,18},{26,30},{30,26},{34,38... | collective-permute-start | bytes 24584 | tf_op jit(solution)/shard_map/ppermute | solution.py:221
  75.0 2.4 %collective-permute-start.14 = (f32[8,256]{1,0:T(8,128)S(1)}, f32[8,256]{1,0:T(8,128)S(1)}, u32[]{:S(2)}, u32[]{:S(2)}) collective-permute-start(f32[8,256]{1,0:T(8,128)S(1)} %slice.12.r0), channel_id=1, source_target_pairs={{2,10},{6,14},{10,2},{14,6},{18,26},{22,30},{26,18},{30,22},{34,42... | collective-permute-start | bytes 24584 | tf_op jit(solution)/shard_map/ppermute | solution.py:221
  77.3 3.5 %collective-permute-start.15 = (f32[8,256]{1,0:T(8,128)S(1)}, f32[8,256]{1,0:T(8,128)S(1)}, u32[]{:S(2)}, u32[]{:S(2)}) collective-permute-start(f32[8,256]{1,0:T(8,128)S(1)} %slice.12.r0), channel_id=1, source_target_pairs={{2,14},{6,10},{10,6},{14,2},{18,30},{22,26},{26,22},{30,18},{34,46... | collective-permute-start | bytes 24584 | tf_op jit(solution)/shard_map/ppermute | solution.py:221
  80.9 2.6 %collective-permute-done.15.r3 = f32[8,256]{1,0:T(8,128)S(1)} collective-permute-done((f32[8,256]{1,0:T(8,128)S(1)}, f32[8,256]{1,0:T(8,128)S(1)}, u32[]{:S(2)}, u32[]{:S(2)}) %collective-permute-start.15) | collective-permute-done | bytes 8224 | tf_op jit(solution)/shard_map/ppermute | solution.py:221
  84.1 2.2 %up_z.1 = (f32[8,256]{1,0:T(8,128)}, f32[8,256]{1,0:T(8,128)}) custom-call(f32[8,256]{1,0:T(8,128)} %copy-done.7, f32[8,256]{1,0:T(8,128)} %copy-done.12, f32[8,256]{1,0:T(8,128)} %copy-done.14, f32[8,256]{1,0:T(8,128)} %copy-done.16, f32[4,136,256]{2,1,0:T(8,128)} %get-tuple-element.25.s, f32[2,128,256]{2,1,0:T(8,128)} %get-tuple-element.26.v), custom_call_target="tpu_custom_call" | custom-call | flops 200000000 | bytes 1000000 | tf_op jit(solution)/shard_map/up_z/pallas_call | solution.py:206
  86.3 1.9 %collective-permute-start.16 = (f32[8,256]{1,0:T(8,128)}, f32[8,256]{1,0:T(8,128)S(1)}, u32[]{:S(2)}, u32[]{:S(2)}) collective-permute-start(f32[8,256]{1,0:T(8,128)} %get-tuple-element.27.r0), channel_id=1, source_target_pairs={{2,18},{6,22},{10,26},{14,30},{18,2},{22,6},{26,10},{30,14},{34,50... | collective-permute-start | bytes 24584 | tf_op jit(solution)/shard_map/ppermute | solution.py:221
  88.2 3.9 %collective-permute-start.17 = (f32[8,256]{1,0:T(8,128)}, f32[8,256]{1,0:T(8,128)S(1)}, u32[]{:S(2)}, u32[]{:S(2)}) collective-permute-start(f32[8,256]{1,0:T(8,128)} %get-tuple-element.27.r0), channel_id=1, source_target_pairs={{2,34},{6,38},{10,42},{14,46},{18,50},{22,54},{26,58},{30,62},{34,... | collective-permute-start | bytes 24584 | tf_op jit(solution)/shard_map/ppermute | solution.py:221
  92.1 3.7 %collective-permute-start.18 = (f32[8,256]{1,0:T(8,128)}, f32[8,256]{1,0:T(8,128)S(1)}, u32[]{:S(2)}, u32[]{:S(2)}) collective-permute-start(f32[8,256]{1,0:T(8,128)} %get-tuple-element.27.r0), channel_id=1, source_target_pairs={{2,50},{6,54},{10,58},{14,62},{18,34},{22,38},{26,42},{30,46},{34,... | collective-permute-start | bytes 24584 | tf_op jit(solution)/shard_map/ppermute | solution.py:221
  95.9 2.0 %collective-permute-done.18.r3 = f32[8,256]{1,0:T(8,128)S(1)} collective-permute-done((f32[8,256]{1,0:T(8,128)}, f32[8,256]{1,0:T(8,128)S(1)}, u32[]{:S(2)}, u32[]{:S(2)}) %collective-permute-start.18) | collective-permute-done | bytes 8224 | tf_op jit(solution)/shard_map/ppermute | solution.py:221
  98.6 2.2 %up_x.1 = (f32[8,256]{1,0:T(8,128)}, f32[8,256]{1,0:T(8,128)}) custom-call(f32[8,256]{1,0:T(8,128)} %get-tuple-element.27.r0, f32[8,256]{1,0:T(8,128)} %copy-done.13, f32[8,256]{1,0:T(8,128)} %copy-done.15, f32[8,256]{1,0:T(8,128)} %copy-done.17, f32[4,136,256]{2,1,0:T(8,128)} %get-tuple-element.28.s, f32[2,128,256]{2,1,0:T(8,128)} %get-tuple-element.29.v), custom_call_target="tpu_custom_call" | custom-call | flops 200000000 | bytes 1000000 | tf_op jit(solution)/shard_map/up_x/pallas_call | solution.py:206
  100.7 2.7 %collective-permute-start.19 = (f32[8,256]{1,0:T(8,128)}, f32[8,256]{1,0:T(8,128)S(1)}, u32[]{:S(2)}, u32[]{:S(2)}) collective-permute-start(f32[8,256]{1,0:T(8,128)} %get-tuple-element.30.e0), channel_id=1, source_target_pairs={{2,66},{6,70},{10,74},{14,78},{18,82},{22,86},{26,90},{30,94},{34,... | collective-permute-start | bytes 24584 | tf_op jit(solution)/shard_map/ppermute | solution.py:221
  103.4 4.4 %collective-permute-start.20 = (f32[8,256]{1,0:T(8,128)}, f32[8,256]{1,0:T(8,128)S(1)}, u32[]{:S(2)}, u32[]{:S(2)}) collective-permute-start(f32[8,256]{1,0:T(8,128)} %get-tuple-element.30.e0), channel_id=1, source_target_pairs={{2,130},{6,134},{10,138},{14,142},{18,146},{22,150},{26,154},{30,1... | collective-permute-start | bytes 24584 | tf_op jit(solution)/shard_map/ppermute | solution.py:221
  107.8 2.5 %collective-permute-start.21 = (f32[8,256]{1,0:T(8,128)}, f32[8,256]{1,0:T(8,128)S(1)}, u32[]{:S(2)}, u32[]{:S(2)}) collective-permute-start(f32[8,256]{1,0:T(8,128)} %get-tuple-element.30.e0), channel_id=1, source_target_pairs={{2,194},{6,198},{10,202},{14,206},{18,210},{22,214},{26,218},{30,2... | collective-permute-start | bytes 24584 | tf_op jit(solution)/shard_map/ppermute | solution.py:221
  110.4 3.3 %collective-permute-done.21.e3 = f32[8,256]{1,0:T(8,128)S(1)} collective-permute-done((f32[8,256]{1,0:T(8,128)}, f32[8,256]{1,0:T(8,128)S(1)}, u32[]{:S(2)}, u32[]{:S(2)}) %collective-permute-start.21) | collective-permute-done | bytes 8224 | tf_op jit(solution)/shard_map/ppermute | solution.py:221
  113.7 0.6 copy-done.10
  114.2 3.1 %last.1 = f32[4,128]{1,0:T(4,128)} custom-call(f32[8,256]{1,0:T(8,128)} %get-tuple-element.30.e0, f32[8,256]{1,0:T(8,128)} %copy-done.8, f32[8,256]{1,0:T(8,128)} %copy-done.9, f32[8,256]{1,0:T(8,128)} %copy-done.10, f32[136,256]{1,0:T(8,128)} %get-tuple-element.22.r0, f32[136,256]{1,0:T(8,128)} %copy-done.3, f32[136,256]{1,0:T(8,128)} %copy-done.1, ...), custom_call_target="tpu_custom_call" | custom-call | flops 200000000 | bytes 1000000 | tf_op jit(solution)/shard_map/last/pallas_call | solution.py:206
  117.4 0.7 slice.10
  118.1 1.3 %collective-permute-start.22 = (f32[2,128]{1,0:T(2,128)S(1)}, f32[2,128]{1,0:T(2,128)S(1)}, u32[]{:S(2)}, u32[]{:S(2)}) collective-permute-start(f32[2,128]{1,0:T(2,128)S(1)} %slice.10), channel_id=1, source_target_pairs={{2,0},{6,4},{10,8},{14,12},{18,16},{22,20},{26,24},{30,28},{34,32}... | collective-permute-start | bytes 3080 | tf_op jit(solution)/shard_map/ppermute | solution.py:266
  119.4 0.8 collective-permute-done.22
  (58 shorter events, 2.9 us)
Async XLA Ops:
  2.6 8.9 %collective-permute-start = (f32[2,144,256]{2,1,0:T(8,128)}, f32[2,144,256]{2,1,0:T(8,128)S(1)}, u32[]{:S(2)}, u32[]{:S(2)}) collective-permute-start(f32[2,144,256]{2,1,0:T(8,128)} %get-tuple-element.19.own), channel_id=1, source_target_pairs={{0,2},{2,0},{4,6},{6,4},{8,10},{10,8},{12,14},{14,12},{16,18},{18,... | collective-permute-start | bytes 884744 | tf_op jit(solution)/shard_map/ppermute | solution.py:239
  5.9 8.6 %collective-permute-start.1 = (f32[2,16,256]{2,1,0:T(8,128)}, f32[2,16,256]{2,1,0:T(8,128)S(1)}, u32[]{:S(2)}, u32[]{:S(2)}) collective-permute-start(f32[2,16,256]{2,1,0:T(8,128)} %get-tuple-element.20), channel_id=1, source_target_pairs={{0,1},{1,0},{2,3},{3,2},{4,5},{5,4},{6,7},{7,6},{8,9},{9,8},{10,11... | collective-permute-start | bytes 98312 | tf_op jit(solution)/shard_map/ppermute | solution.py:240
  11.1 7.5 %collective-permute-start.2 = (f32[2,16,256]{2,1,0:T(8,128)}, f32[2,16,256]{2,1,0:T(8,128)S(1)}, u32[]{:S(2)}, u32[]{:S(2)}) collective-permute-start(f32[2,16,256]{2,1,0:T(8,128)} %get-tuple-element.20), channel_id=1, source_target_pairs={{0,3},{1,2},{2,1},{3,0},{4,7},{5,6},{6,5},{7,4},{8,11},{9,10},{10,... | collective-permute-start | bytes 98312 | tf_op jit(solution)/shard_map/ppermute | solution.py:241
  11.5 0.7 copy-start
  14.5 4.1 %copy-start.4 = (f32[2,16,256]{2,1,0:T(8,128)}, f32[2,16,256]{2,1,0:T(8,128)S(1)}, u32[]{:S(2)}) copy-start(f32[2,16,256]{2,1,0:T(8,128)S(1)} %collective-permute-done.1.same) | copy-start | bytes 98308
  18.6 0.6 copy-start.5
  21.5 6.9 %collective-permute-start.3 = (f32[136,256]{1,0:T(8,128)}, f32[136,256]{1,0:T(8,128)S(1)}, u32[]{:S(2)}, u32[]{:S(2)}) collective-permute-start(f32[136,256]{1,0:T(8,128)} %offset.1.r0), channel_id=1, source_target_pairs={{0,4},{2,6},{4,0},{6,2},{8,12},{10,14},{12,8},{14,10},{16,20},{18,... | collective-permute-start | bytes 417800 | tf_op jit(solution)/shard_map/ppermute | solution.py:221
  22.2 6.3 %collective-permute-start.4 = (f32[136,256]{1,0:T(8,128)}, f32[136,256]{1,0:T(8,128)S(1)}, u32[]{:S(2)}, u32[]{:S(2)}) collective-permute-start(f32[136,256]{1,0:T(8,128)} %offset.1.r0), channel_id=1, source_target_pairs={{0,8},{2,10},{4,12},{6,14},{8,0},{10,2},{12,4},{14,6},{16,24},{18,... | collective-permute-start | bytes 417800 | tf_op jit(solution)/shard_map/ppermute | solution.py:221
  23.7 9.8 %collective-permute-start.5 = (f32[136,256]{1,0:T(8,128)}, f32[136,256]{1,0:T(8,128)S(1)}, u32[]{:S(2)}, u32[]{:S(2)}) collective-permute-start(f32[136,256]{1,0:T(8,128)} %offset.1.r0), channel_id=1, source_target_pairs={{0,12},{2,14},{4,8},{6,10},{8,4},{10,6},{12,0},{14,2},{16,28},{18,... | collective-permute-start | bytes 417800 | tf_op jit(solution)/shard_map/ppermute | solution.py:221
  28.4 5.1 %copy-start.18 = (f32[136,256]{1,0:T(8,128)}, f32[136,256]{1,0:T(8,128)S(1)}, u32[]{:S(2)}) copy-start(f32[136,256]{1,0:T(8,128)S(1)} %collective-permute-done.3.r1) | copy-start | bytes 417796
  28.5 4.9 %copy-start.20 = (f32[136,256]{1,0:T(8,128)}, f32[136,256]{1,0:T(8,128)S(1)}, u32[]{:S(2)}) copy-start(f32[136,256]{1,0:T(8,128)S(1)} %collective-permute-done.4.r2) | copy-start | bytes 417796
  33.5 0.7 copy-start.22
  36.6 4.1 %collective-permute-start.6 = (f32[136,256]{1,0:T(8,128)}, f32[136,256]{1,0:T(8,128)S(1)}, u32[]{:S(2)}, u32[]{:S(2)}) collective-permute-start(f32[136,256]{1,0:T(8,128)} %get-tuple-element.21.r0), channel_id=1, source_target_pairs={{0,16},{2,18},{4,20},{6,22},{8,24},{10,26},{12,28},{14,30},{16,0},... | collective-permute-start | bytes 417800 | tf_op jit(solution)/shard_map/ppermute | solution.py:221
  37.8 6.6 %collective-permute-start.7 = (f32[136,256]{1,0:T(8,128)}, f32[136,256]{1,0:T(8,128)S(1)}, u32[]{:S(2)}, u32[]{:S(2)}) collective-permute-start(f32[136,256]{1,0:T(8,128)} %get-tuple-element.21.r0), channel_id=1, source_target_pairs={{0,32},{2,34},{4,36},{6,38},{8,40},{10,42},{12,44},{14,46},{16,48}... | collective-permute-start | bytes 417800 | tf_op jit(solution)/shard_map/ppermute | solution.py:221
  40.3 5.6 %collective-permute-start.8 = (f32[136,256]{1,0:T(8,128)}, f32[136,256]{1,0:T(8,128)S(1)}, u32[]{:S(2)}, u32[]{:S(2)}) collective-permute-start(f32[136,256]{1,0:T(8,128)} %get-tuple-element.21.r0), channel_id=1, source_target_pairs={{0,48},{2,50},{4,52},{6,54},{8,56},{10,58},{12,60},{14,62},{16,32}... | collective-permute-start | bytes 417800 | tf_op jit(solution)/shard_map/ppermute | solution.py:221
  40.7 5.2 %copy-start.19 = (f32[136,256]{1,0:T(8,128)}, f32[136,256]{1,0:T(8,128)S(1)}, u32[]{:S(2)}) copy-start(f32[136,256]{1,0:T(8,128)S(1)} %collective-permute-done.6.r1) | copy-start | bytes 417796
  44.5 1.5 %copy-start.21 = (f32[136,256]{1,0:T(8,128)}, f32[136,256]{1,0:T(8,128)S(1)}, u32[]{:S(2)}) copy-start(f32[136,256]{1,0:T(8,128)S(1)} %collective-permute-done.7.r2) | copy-start | bytes 417796
  45.9 0.7 copy-start.23
  49.1 5.6 %collective-permute-start.10 = (f32[136,256]{1,0:T(8,128)}, f32[136,256]{1,0:T(8,128)S(1)}, u32[]{:S(2)}, u32[]{:S(2)}) collective-permute-start(f32[136,256]{1,0:T(8,128)} %get-tuple-element.22.r0), channel_id=1, source_target_pairs={{0,128},{2,130},{4,132},{6,134},{8,136},{10,138},{12,140},{14,142}... | collective-permute-start | bytes 417800 | tf_op jit(solution)/shard_map/ppermute | solution.py:221
  52.0 5.3 %collective-permute-start.11 = (f32[136,256]{1,0:T(8,128)}, f32[136,256]{1,0:T(8,128)S(1)}, u32[]{:S(2)}, u32[]{:S(2)}) collective-permute-start(f32[136,256]{1,0:T(8,128)} %get-tuple-element.22.r0), channel_id=1, source_target_pairs={{0,192},{2,194},{4,196},{6,198},{8,200},{10,202},{12,204},{14,206}... | collective-permute-start | bytes 417800 | tf_op jit(solution)/shard_map/ppermute | solution.py:221
  52.8 4.6 %collective-permute-start.9 = (f32[136,256]{1,0:T(8,128)}, f32[136,256]{1,0:T(8,128)S(1)}, u32[]{:S(2)}, u32[]{:S(2)}) collective-permute-start(f32[136,256]{1,0:T(8,128)} %get-tuple-element.22.r0), channel_id=1, source_target_pairs={{0,64},{2,66},{4,68},{6,70},{8,72},{10,74},{12,76},{14,78},{16,80}... | collective-permute-start | bytes 417800 | tf_op jit(solution)/shard_map/ppermute | solution.py:221
  54.7 2.6 %copy-start.1 = (f32[136,256]{1,0:T(8,128)}, f32[136,256]{1,0:T(8,128)S(1)}, u32[]{:S(2)}) copy-start(f32[136,256]{1,0:T(8,128)S(1)} %collective-permute-done.10.r2) | copy-start | bytes 417796
  57.3 0.7 copy-start.2
  57.3 0.7 copy-start.3
  61.5 8.7 %collective-permute-start.12 = (f32[40,256]{1,0:T(8,128)}, f32[40,256]{1,0:T(8,128)S(1)}, u32[]{:S(2)}, u32[]{:S(2)}) collective-permute-start(f32[40,256]{1,0:T(8,128)} %turn.1), channel_id=1, source_target_pairs={{0,2},{4,6},{8,10},{12,14},{16,18},{20,22},{24,26},{28,30},{32,34}... | collective-permute-start | bytes 122888 | tf_op jit(solution)/shard_map/ppermute | solution.py:255
  70.2 16.1 %copy-start.6 = (f32[40,256]{1,0:T(8,128)}, f32[40,256]{1,0:T(8,128)S(1)}, u32[]{:S(2)}) copy-start(f32[40,256]{1,0:T(8,128)S(1)} %collective-permute-done.12.d) | copy-start | bytes 122884
  70.2 13.3 %copy-start.7 = (f32[8,256]{1,0:T(8,128)}, f32[8,256]{1,0:T(8,128)S(1)}, u32[]{:S(2)}) copy-start(f32[8,256]{1,0:T(8,128)S(1)} %slice.12.r0) | copy-start | bytes 24580
  70.2 10.7 %collective-permute-start.13 = (f32[8,256]{1,0:T(8,128)S(1)}, f32[8,256]{1,0:T(8,128)S(1)}, u32[]{:S(2)}, u32[]{:S(2)}) collective-permute-start(f32[8,256]{1,0:T(8,128)S(1)} %slice.12.r0), channel_id=1, source_target_pairs={{2,6},{6,2},{10,14},{14,10},{18,22},{22,18},{26,30},{30,26},{34,38... | collective-permute-start | bytes 24584 | tf_op jit(solution)/shard_map/ppermute | solution.py:221
  75.0 5.9 %collective-permute-start.14 = (f32[8,256]{1,0:T(8,128)S(1)}, f32[8,256]{1,0:T(8,128)S(1)}, u32[]{:S(2)}, u32[]{:S(2)}) collective-permute-start(f32[8,256]{1,0:T(8,128)S(1)} %slice.12.r0), channel_id=1, source_target_pairs={{2,10},{6,14},{10,2},{14,6},{18,26},{22,30},{26,18},{30,22},{34,42... | collective-permute-start | bytes 24584 | tf_op jit(solution)/shard_map/ppermute | solution.py:221
  77.3 6.2 %collective-permute-start.15 = (f32[8,256]{1,0:T(8,128)S(1)}, f32[8,256]{1,0:T(8,128)S(1)}, u32[]{:S(2)}, u32[]{:S(2)}) collective-permute-start(f32[8,256]{1,0:T(8,128)S(1)} %slice.12.r0), channel_id=1, source_target_pairs={{2,14},{6,10},{10,6},{14,2},{18,30},{22,26},{26,22},{30,18},{34,46... | collective-permute-start | bytes 24584 | tf_op jit(solution)/shard_map/ppermute | solution.py:221
  80.9 2.6 %copy-start.12 = (f32[8,256]{1,0:T(8,128)}, f32[8,256]{1,0:T(8,128)S(1)}, u32[]{:S(2)}) copy-start(f32[8,256]{1,0:T(8,128)S(1)} %collective-permute-done.13.r1) | copy-start | bytes 24580
  80.9 2.6 %copy-start.14 = (f32[8,256]{1,0:T(8,128)}, f32[8,256]{1,0:T(8,128)S(1)}, u32[]{:S(2)}) copy-start(f32[8,256]{1,0:T(8,128)S(1)} %collective-permute-done.14.r2) | copy-start | bytes 24580
  83.5 0.6 copy-start.16
  86.3 9.6 %collective-permute-start.16 = (f32[8,256]{1,0:T(8,128)}, f32[8,256]{1,0:T(8,128)S(1)}, u32[]{:S(2)}, u32[]{:S(2)}) collective-permute-start(f32[8,256]{1,0:T(8,128)} %get-tuple-element.27.r0), channel_id=1, source_target_pairs={{2,18},{6,22},{10,26},{14,30},{18,2},{22,6},{26,10},{30,14},{34,50... | collective-permute-start | bytes 24584 | tf_op jit(solution)/shard_map/ppermute | solution.py:221
  88.2 7.7 %collective-permute-start.17 = (f32[8,256]{1,0:T(8,128)}, f32[8,256]{1,0:T(8,128)S(1)}, u32[]{:S(2)}, u32[]{:S(2)}) collective-permute-start(f32[8,256]{1,0:T(8,128)} %get-tuple-element.27.r0), channel_id=1, source_target_pairs={{2,34},{6,38},{10,42},{14,46},{18,50},{22,54},{26,58},{30,62},{34,... | collective-permute-start | bytes 24584 | tf_op jit(solution)/shard_map/ppermute | solution.py:221
  92.1 5.8 %collective-permute-start.18 = (f32[8,256]{1,0:T(8,128)}, f32[8,256]{1,0:T(8,128)S(1)}, u32[]{:S(2)}, u32[]{:S(2)}) collective-permute-start(f32[8,256]{1,0:T(8,128)} %get-tuple-element.27.r0), channel_id=1, source_target_pairs={{2,50},{6,54},{10,58},{14,62},{18,34},{22,38},{26,42},{30,46},{34,... | collective-permute-start | bytes 24584 | tf_op jit(solution)/shard_map/ppermute | solution.py:221
  95.9 2.1 %copy-start.13 = (f32[8,256]{1,0:T(8,128)}, f32[8,256]{1,0:T(8,128)S(1)}, u32[]{:S(2)}) copy-start(f32[8,256]{1,0:T(8,128)S(1)} %collective-permute-done.16.r1) | copy-start | bytes 24580
  95.9 2.0 %copy-start.15 = (f32[8,256]{1,0:T(8,128)}, f32[8,256]{1,0:T(8,128)S(1)}, u32[]{:S(2)}) copy-start(f32[8,256]{1,0:T(8,128)S(1)} %collective-permute-done.17.r2) | copy-start | bytes 24580
  98.0 0.6 copy-start.17
  100.7 9.6 %collective-permute-start.19 = (f32[8,256]{1,0:T(8,128)}, f32[8,256]{1,0:T(8,128)S(1)}, u32[]{:S(2)}, u32[]{:S(2)}) collective-permute-start(f32[8,256]{1,0:T(8,128)} %get-tuple-element.30.e0), channel_id=1, source_target_pairs={{2,66},{6,70},{10,74},{14,78},{18,82},{22,86},{26,90},{30,94},{34,... | collective-permute-start | bytes 24584 | tf_op jit(solution)/shard_map/ppermute | solution.py:221
  103.4 6.9 %collective-permute-start.20 = (f32[8,256]{1,0:T(8,128)}, f32[8,256]{1,0:T(8,128)S(1)}, u32[]{:S(2)}, u32[]{:S(2)}) collective-permute-start(f32[8,256]{1,0:T(8,128)} %get-tuple-element.30.e0), channel_id=1, source_target_pairs={{2,130},{6,134},{10,138},{14,142},{18,146},{22,150},{26,154},{30,1... | collective-permute-start | bytes 24584 | tf_op jit(solution)/shard_map/ppermute | solution.py:221
  107.8 5.8 %collective-permute-start.21 = (f32[8,256]{1,0:T(8,128)}, f32[8,256]{1,0:T(8,128)S(1)}, u32[]{:S(2)}, u32[]{:S(2)}) collective-permute-start(f32[8,256]{1,0:T(8,128)} %get-tuple-element.30.e0), channel_id=1, source_target_pairs={{2,194},{6,198},{10,202},{14,206},{18,210},{22,214},{26,218},{30,2... | collective-permute-start | bytes 24584 | tf_op jit(solution)/shard_map/ppermute | solution.py:221
  110.3 3.3 %copy-start.8 = (f32[8,256]{1,0:T(8,128)}, f32[8,256]{1,0:T(8,128)S(1)}, u32[]{:S(2)}) copy-start(f32[8,256]{1,0:T(8,128)S(1)} %collective-permute-done.19.e1) | copy-start | bytes 24580
  110.3 3.3 %copy-start.9 = (f32[8,256]{1,0:T(8,128)}, f32[8,256]{1,0:T(8,128)S(1)}, u32[]{:S(2)}) copy-start(f32[8,256]{1,0:T(8,128)S(1)} %collective-permute-done.20.e2) | copy-start | bytes 24580
  113.6 0.6 copy-start.10
  118.1 2.1 %collective-permute-start.22 = (f32[2,128]{1,0:T(2,128)S(1)}, f32[2,128]{1,0:T(2,128)S(1)}, u32[]{:S(2)}, u32[]{:S(2)}) collective-permute-start(f32[2,128]{1,0:T(2,128)S(1)} %slice.10), channel_id=1, source_target_pairs={{2,0},{6,4},{10,8},{14,12},{18,16},{22,20},{26,24},{30,28},{34,32}... | collective-permute-start | bytes 3080 | tf_op jit(solution)/shard_map/ppermute | solution.py:266
  119.3 0.8 copy-start.11

commit v2 on v1

v2 whole, which is shorter than its diff:
```python
import functools
import math

import jax
import jax.numpy as jnp
from jax import lax
from jax.experimental import pallas as pl
from jax.experimental.pallas import tpu as pltpu
from jax.sharding import PartitionSpec as P


B = 128
W2 = 2 * B
NANG = 64
WAVENUMBER = 0.8
FIELDS = 8
ROWS = B + FIELDS
F32 = jnp.float32
BF16 = jnp.bfloat16


def split(v):
    hi = v.astype(BF16)
    return hi, (v - hi.astype(F32)).astype(BF16)


def wide(part):
    re, im = part[:, :B], part[:, B:]
    return jnp.concatenate([part, jnp.concatenate([-im, re], axis=1)], axis=0)


def weights(t):
    hi, lo = split(t)
    return wide(hi), wide(lo)


def dot(a, b):
    return jnp.dot(a, b, preferred_element_type=F32)


def mul(v, w):
    hi, lo = split(v)
    return (dot(lo, w[0]) + dot(hi, w[1])) + dot(hi, w[0])


def mulv(v, w):
    n = v.shape[0]
    hi, lo = split(v)
    both = jnp.concatenate([hi, lo], axis=0)
    a, b = dot(both, w[0]), dot(both, w[1])
    return (a[n:] + b[:n]) + a[:n]


def place(shift):
    d = lax.axis_index("depth")
    core = d & 1
    at = (d >> shift) & 3
    return jnp.where(core == 0, at, 3 - at)


def waves(direction, depth, lane):
    arg = WAVENUMBER * (jnp.sin(direction) * lane + jnp.cos(direction) * depth)
    return jnp.cos(arg), jnp.sin(arg)


def eights():
    row = lax.broadcasted_iota(jnp.int32, (FIELDS, B), 0)
    lane = lax.broadcasted_iota(jnp.int32, (FIELDS, B), 1).astype(F32)
    return row, lane, (row & 1) == 1


def prep_kernel(angles, choice, contrast, adj, blocks, own, oth, ang, pick, con, src, raw, sem):
    t = lax.axis_index("src")
    first = (lax.axis_index("depth") * 2).astype(F32)
    moves = ((blocks.at[:, t], raw), (choice, pick), (angles, ang), (contrast, con), (adj, src))
    copies = [pltpu.make_async_copy(f, g, sem.at[n]) for n, (f, g) in enumerate(moves)]
    for c in copies:
        c.start()
    row, lane, odd = eights()
    for c in copies[1:]:
        c.wait()
    turn = jnp.where(odd, jnp.full((FIELDS, B), ang[1]), jnp.full((FIELDS, B), ang[0])).astype(F32)
    is_f, is_a = row < 2, (row >= 4) & (row < 6)
    zero = jnp.zeros((FIELDS, B), F32)

    def tiled(line, tile):
        return jnp.where(tile == 0, line[:, :B], line[:, B:])

    for l in range(2):
        inc = waves(turn * (2.0 * math.pi / NANG), first + float(l), lane)
        own_con = jnp.broadcast_to(tiled(con[pl.ds(l, 1), :], t), (FIELDS, B))
        for p in range(2):
            part = slice(p * B, (p + 1) * B)
            lines = [src[p, i, pl.ds(l, 1), :] for i in range(2)]
            a = jnp.where(odd, tiled(lines[1], t), tiled(lines[0], t))
            own[l, B : B + 8, part] = jnp.where(is_f, inc[p] * own_con, jnp.where(is_a, a, zero))
            own[l, B + 8 : B + 16, part] = jnp.where(is_f, inc[p], zero)
            own[l, B + 16 : B + 24, part] = own_con
            for i in range(2):
                oth[2 * l + i : 2 * l + i + 1, part] = tiled(lines[i], 1 - t)
    for p in range(2):
        oth[4:8, p * B : (p + 1) * B] = jnp.full((4, B), ang[p]).astype(F32)
    copies[0].wait()
    for l in range(2):
        for p in range(2):
            own[l, :B, p * B : (p + 1) * B] = raw[pick[l], p].T


def chip_kernel(own, peer, x):
    core = lax.axis_index("depth") & 1
    g = [(own if s < 2 else peer)[(s & 1) ^ core, :B, :] for s in range(4)]
    x01 = mul(g[0], weights(g[1]))
    x23 = mul(g[2], weights(g[3]))
    x[...] = mul(x01, weights(x23))


def offset_kernel(own, peer, same, cross, c, hi):
    d = lax.axis_index("depth")
    core = d & 1
    row, lane, odd = eights()
    is_f, is_a = (row >= 2) & (row < 4), row >= 6
    zero = jnp.zeros((FIELDS, B), F32)
    v = jnp.zeros((FIELDS, W2), F32)
    for k in range(4):
        a, b = (own, same) if k < 2 else (peer, cross)
        l = k & 1
        depth = ((d >> 1) * 4 + ((k >> 1) ^ core) * 2 + l).astype(F32)
        turn = jnp.where(odd, b[4:5, B:], b[4:5, :B])
        inc = waves(turn * (2.0 * math.pi / NANG), depth, lane)
        con = a[l, B + 16 : B + 24, :B]
        h, n = [], []
        for p in range(2):
            part = slice(p * B, (p + 1) * B)
            line = jnp.where(odd, b[2 * l + 1 : 2 * l + 2, part], b[2 * l : 2 * l + 1, part])
            h.append(a[l, B : B + 8, part] + jnp.where(is_f, inc[p] * con, jnp.where(is_a, line, zero)))
            n.append(a[l, B + 8 : B + 16, part] + jnp.where(is_f, inc[p], zero))
        h = jnp.concatenate(h, axis=1)
        hi[k, :8, :] = h
        hi[k, 8:, :] = jnp.concatenate(n, axis=1)
        v = mulv(v + h, weights(a[l, :B, :]))
    c[...] = jnp.where(core == 0, v, 0.0)


def pair_kernel(shift, mine, theirs, x, second):
    late = (place(shift) & 1) == 1
    a = jnp.where(late, theirs[...], mine[...])
    b = jnp.where(late, mine[...], theirs[...])
    second[...] = b
    x[...] = mul(a, weights(b))


def pair_rows_kernel(shift, mine, theirs, second, c):
    late = (place(shift) & 1) == 1
    a = jnp.where(late, theirs[...], mine[...])
    b = jnp.where(late, mine[...], theirs[...])
    c[...] = mulv(a, weights(second[...])) + b


def quad_kernel(shift, mine, theirs, c_mine, c_theirs, mate, c_mate, x, p, second):
    q = place(shift)
    late, odd = q >= 2, (q & 1) == 1
    a = jnp.where(late, theirs[...], mine[...])
    b = jnp.where(late, mine[...], theirs[...])
    ca = jnp.where(late, c_theirs[...], c_mine[...])
    cb = jnp.where(late, c_mine[...], c_theirs[...])
    w = weights(b)
    x[:B, :] = mul(a, w)
    x[B:, :] = mulv(ca, w) + cb
    second[...] = b
    row = lax.broadcasted_iota(jnp.int32, (B, W2), 0)
    col = lax.broadcasted_iota(jnp.int32, (B, W2), 1)
    base = jnp.where(late, a, jnp.where(row == col, 1.0, 0.0))
    c_base = jnp.where(late, ca, 0.0)
    w = weights(mate[...])
    p[:B, :] = jnp.where(odd, mul(base, w), base)
    p[B:, :] = jnp.where(odd, mulv(c_base, w) + c_mate[...], c_base)


def quad_rows_kernel(shift, mine, theirs, second, mate, c_mate, total, part):
    q = place(shift)
    late, odd = q >= 2, (q & 1) == 1
    a = jnp.where(late, theirs[...], mine[...])
    b = jnp.where(late, mine[...], theirs[...])
    total[...] = mulv(a, weights(second[...])) + b
    base = jnp.where(late, a, 0.0)
    part[...] = jnp.where(odd, mulv(base, weights(mate[...])) + c_mate[...], base)


def level_kernel(shift, r0, r1, r2, r3, x, s, p, v):
    q = place(shift)
    for k, r in enumerate((r0, r1, r2, r3)):
        s[q ^ k] = r[...]
    row = lax.broadcasted_iota(jnp.int32, (ROWS, W2), 0)
    col = lax.broadcasted_iota(jnp.int32, (ROWS, W2), 1)
    tail = row >= B

    def step(a, b):
        return mul(a, weights(b[:B])) + jnp.where(tail, b, 0.0)

    s0, s1, s2, s3 = (s[k] for k in range(4))
    x01 = step(s0, s1)
    x23 = step(s2, s3)
    x[...] = step(x01, x23)
    x012 = step(x01, s2)
    one = jnp.where((row == col) & (row < B), 1.0, 0.0)
    p[...] = jnp.where(q == 0, one, jnp.where(q == 1, s0, jnp.where(q == 2, x01, x012)))
    v[0] = x23[:B]
    v[1] = mul(s1[:B], weights(x23[:B]))


def turn_kernel(r0, r1, r2, r3, pz, px, own, peer, hi, out, s):
    q = place(5)
    for k, r in enumerate((r0, r1, r2, r3)):
        s[q ^ k] = r[...]
    a = jnp.where(q > 0, s[0, B:, :], 0.0)
    for k in (1, 2):
        a = jnp.where(q > k, mulv(a, weights(s[k, :B, :])) + s[k, B:, :], a)
    for p in (px, pz):
        a = mulv(a, weights(p[:B, :])) + p[B:, :]
    ws, ds = [], []
    for k in range(4):
        w = weights((own if k < 2 else peer)[k & 1, :B, :])
        a = mulv(a + hi[k, :8, :], w)
        ws.append(w)
        ds.append(a)
        out[8 + 8 * k : 16 + 8 * k, :] = a
    u = ds[3]
    for k in (2, 1, 0):
        u = ds[k] + mulv(u, ws[k])
    out[:8, :] = u


def gather_kernel(shift, r0, r1, r2, r3, s, v, total, part, e):
    q = place(shift)
    for k, r in enumerate((r0, r1, r2, r3)):
        e[q ^ k] = r[...]
    total[...] = (
        (mulv(e[0], weights(v[1])) + mulv(e[1], weights(v[0])))
        + mulv(e[2], weights(s[3, :B, :]))
        + e[3]
    )
    c = jnp.where(q > 0, e[0], 0.0)
    for k in (1, 2):
        c = jnp.where(q > k, mulv(c, weights(s[k, :B, :])) + e[k], c)
    part[...] = c


def last_kernel(e0, e1, e2, e3, r0, r1, r2, r3, px, pz, cx, cz, own, peer, hi, d, grad, e, s):
    q = place(5)
    for k, (f, r) in enumerate(((e0, r0), (e1, r1), (e2, r2), (e3, r3))):
        e[q ^ k] = f[...]
        s[q ^ k] = r[...]
    u = jnp.where(q > 0, e[0], 0.0)
    for k in (1, 2):
        u = jnp.where(q > k, mulv(u, weights(s[k, :B, :])) + e[k], u)
    for p, c in ((px, cx), (pz, cz)):
        u = mulv(u, weights(p[:B, :])) + c[...]
    for k in (3, 2, 1, 0):
        g = peer if k < 2 else own
        u = d[8 + 8 * k : 16 + 8 * k, :] + mulv(u, weights(g[k & 1, :B, :]))
        f = u + hi[k ^ 2, 8:, :]
        prod = f[:4] * f[4:]
        tot = jnp.sum(prod, axis=0, keepdims=True)
        grad[k : k + 1, :] = (tot[:, :B] - tot[:, B:]) * 0.25


def call(kernel, outs, *args, scratch=(), in_specs=None):
    shapes = [jax.ShapeDtypeStruct(o, F32) for o in outs]
    vm = pl.BlockSpec(memory_space=pltpu.VMEM)
    got = pl.pallas_call(
        kernel,
        out_shape=shapes,
        in_specs=in_specs or [vm] * len(args),
        out_specs=[vm] * len(outs),
        scratch_shapes=list(scratch),
        compiler_params=pltpu.CompilerParams(vmem_limit_bytes=8 << 20),
        cost_estimate=pl.CostEstimate(flops=200_000_000, bytes_accessed=1_000_000, transcendentals=0),
    )(*args)
    return got[0] if len(outs) == 1 else got


def flip(value, bit, depth):
    return lax.ppermute(value, "depth", [(i, i ^ bit) for i in range(depth)])


def gather4(value, bit, depth):
    return [value] + [flip(value, k * bit, depth) for k in (1, 2, 3)]


def per_device(angles, factor_choice, contrast, adjoint_source, inverse_blocks):
    depth = lax.axis_size("depth")
    core = lax.axis_index("depth") & 1
    own, oth = call(
        prep_kernel,
        [(2, B + 24, W2), (8, W2)],
        *[pltpu.with_memory_space_constraint(v, pltpu.HBM)
          for v in (angles, factor_choice, contrast, adjoint_source, inverse_blocks)],
        in_specs=[pl.BlockSpec(memory_space=pltpu.HBM)] * 5,
        scratch=[
            pltpu.SMEM((2,), jnp.int32),
            pltpu.SMEM((2,), jnp.int32),
            pltpu.VMEM((2, W2), F32),
            pltpu.VMEM((2, 2, 2, W2), F32),
            pltpu.VMEM((2, 2, B, B), F32),
            pltpu.SemaphoreType.DMA((5,)),
        ],
    )
    peer = flip(own, 1, depth)
    xm = call(chip_kernel, [(B, W2)], own, peer)
    mate = flip(xm, 2, depth)
    same = lax.ppermute(oth, "src", [(0, 1), (1, 0)])
    across = [(2 * i + t, 2 * (i ^ 1) + (1 - t)) for i in range(depth) for t in range(2)]
    cross = lax.ppermute(oth, ("depth", "src"), across)
    x2, s1 = call(functools.partial(pair_kernel, 1), [(B, W2)] * 2, xm, mate)
    x2_far = flip(x2, 4, depth)
    rows = (FIELDS, W2)
    c, hi = call(offset_kernel, [rows, (4, 16, W2)], own, peer, same, cross)
    c_mate = flip(c, 2, depth)
    c2 = call(functools.partial(pair_rows_kernel, 1), [rows], c, c_mate, s1)
    c2_far = flip(c2, 4, depth)
    x, pz, s2 = call(
        functools.partial(quad_kernel, 1), [(ROWS, W2), (ROWS, W2), (B, W2)],
        x2, x2_far, c2, c2_far, mate, c_mate,
    )
    outs = [(ROWS, W2), (4, ROWS, W2), (ROWS, W2), (2, B, W2)]
    x, sx, px, vx = call(functools.partial(level_kernel, 3), outs, *gather4(x, 8, depth))
    ry = gather4(x, 32, depth)
    big = pltpu.VMEM((4, ROWS, W2), F32)
    small = pltpu.VMEM((4, FIELDS, W2), F32)
    sent = call(turn_kernel, [(40, W2)], *ry, pz, px, own, peer, hi, scratch=[big])
    d = flip(sent, 1, depth)
    e = d[:FIELDS]
    e_mate = flip(e, 2, depth)
    e2 = call(functools.partial(pair_rows_kernel, 1), [rows], e, e_mate, s1)
    e2_far = flip(e2, 4, depth)
    e, cz = call(functools.partial(quad_rows_kernel, 1), [rows, rows], e2, e2_far, s2, mate, e_mate)
    ex = gather4(e, 8, depth)
    e, cx = call(functools.partial(gather_kernel, 3), [rows, rows], *ex, sx, vx, scratch=[small])
    ey = gather4(e, 32, depth)
    grad = call(
        last_kernel, [(4, B)], *ey, *ry, px, pz, cx, cz, own, peer, hi, d,
        scratch=[small, big],
    )
    back = flip(grad[:2], 1, depth)
    return jnp.where(core == 0, back, grad[2:])


def solution(mesh):
    placed = (
        P("src"),
        P("depth"),
        P("depth", None),
        P(None, "src", "depth", None),
        P("depth", None, None, None, None),
    )
    return jax.shard_map(
        per_device, mesh=mesh, in_specs=placed, out_specs=P("depth", "src"), check_vma=False
    )
```

time: 121 us -> 87.1 us (0.72)
  Pallas kernels: 23 us -> 6.9 us
  starting transfers between devices: 52.4 us -> 45.4 us
  local copies, waits for them, and re-layouts: 5.82 us -> 0.01 us
  waiting for transfers between devices: 38.7 us -> 34 us
    pallas_call x9 -> x12, Pallas kernels: 23 us -> 6.9 us  [call(): pl.pallas_call(kernel, out_shape=shapes, in_specs=in_specs or [vm] * len(...]
    ppermute x22, starting transfers between devices: 47.2 us -> 40.6 us  [the longest x21 38.5 us: flip(): return lax.ppermute(value, 'depth', [(i, i ^ bit) for i in range(depth)])]
    unnamed x48 -> x0, local copies, waits for them, and re-layouts: 5.15 us -> none
    ppermute x22, waiting for transfers between devices: 38.7 us -> 33.6 us  [the longest x21 29.2 us: flip(): return lax.ppermute(value, 'depth', [(i, i ^ bit) for i in range(depth)])]
  transfers between devices with their start and end apart: 23 -> 23, of which waited for: 14 -> 19; matrix products, arithmetic and copies ran while one was open for 0% -> 0% of each run, Pallas kernels for 2% -> 1%
where the time goes in v2:
time: 87.1 us; the launch traced here: 87 us
  starting transfers between devices  45.4 us (52%)
  waiting for transfers between devices  34 us (39%)
  Pallas kernels  6.9 us (8%)
    ppermute x21, starting transfers between devices, flip(): return lax.ppermute(value, 'depth', [(i, i ^ bit) for i in range(depth)])  38.5 us
    ppermute x21, waiting for transfers between devices, flip(): return lax.ppermute(value, 'depth', [(i, i ^ bit) for i in range(depth)])  29.2 us
    pallas_call x12, Pallas kernels, call(): pl.pallas_call(kernel, out_shape=shapes, in_specs=in_specs or [vm] * len(...  6.9 us
    ppermute x1, starting transfers between devices, per_device(): same = lax.ppermute(oth, 'src', [(0, 1), (1, 0)])  4.75 us
    ppermute x1, waiting for transfers between devices, per_device(): cross = lax.ppermute(oth, ('depth', 'src'), across)  4.44 us
    ppermute x1, starting transfers between devices, per_device(): cross = lax.ppermute(oth, ('depth', 'src'), across)  2.12 us
  transfers between devices with their start and end apart: 23, of which 19 were waited for; matrix products, arithmetic and copies ran while one was open for 0% of the time, Pallas kernels for 1%

profile of v2, /device:TPU:1, one launch (start us, length us, event | category | flops | bytes accessed | tf_op | source)
XLA Modules:
  0.0 87.0 jit_solution(17304044157368897114)
XLA Ops:
  0.0 1.1 %shard_map.55 = (f32[2,152,256]{2,1,0:T(8,128)S(1)}, f32[8,256]{1,0:T(8,128)S(1)}) custom-call(s32[2]{0:T(128)} %angles.1, s32[2]{0:T(128)} %choice.1, f32[2,256]{1,0:T(2,128)} %contrast.1, f32[2,2,2,256]{3,2,1,0:T(2,128)} %adj.1, f32[2,2,2,128,128]{4,3,2,1,0:T(8,128)} %blocks.1), custom_call_target="tpu_custom_call" | custom-call | flops 200000000 | bytes 1000000 | tf_op jit(solution)/shard_map/pallas_call | solution.py:270
  1.1 3.3 %collective-permute-start = (f32[2,152,256]{2,1,0:T(8,128)S(1)}, f32[2,152,256]{2,1,0:T(8,128)S(1)}, u32[]{:S(2)}, u32[]{:S(2)}) collective-permute-start(f32[2,152,256]{2,1,0:T(8,128)S(1)} %get-tuple-element.22.own), channel_id=1, source_target_pairs={{0,2},{2,0},{4,6},{6,4},{8,10},{10,8},{12,14},{14,12},{16,18},{18,... | collective-permute-start | bytes 933896 | tf_op jit(solution)/shard_map/ppermute | solution.py:283
  4.4 1.2 %collective-permute-done.peer = f32[2,152,256]{2,1,0:T(8,128)S(1)} collective-permute-done((f32[2,152,256]{2,1,0:T(8,128)S(1)}, f32[2,152,256]{2,1,0:T(8,128)S(1)}, u32[]{:S(2)}, u32[]{:S(2)}) %collective-permute-start) | collective-permute-done | bytes 311328 | tf_op jit(solution)/shard_map/ppermute | solution.py:283
  5.7 0.5 shard_map.56.mine
  6.3 4.7 %collective-permute-done.1.theirs.mate = f32[128,256]{1,0:T(8,128)S(1)} collective-permute-done((f32[128,256]{1,0:T(8,128)S(1)}, f32[128,256]{1,0:T(8,128)S(1)}, u32[]{:S(2)}, u32[]{:S(2)}) %collective-permute-start.1) | collective-permute-done | bytes 131104 | tf_op jit(solution)/shard_map/ppermute | solution.py:283
  11.0 0.2 shard_map.57
  11.2 1.7 %collective-permute-start.2 = (f32[128,256]{1,0:T(8,128)S(1)}, f32[128,256]{1,0:T(8,128)S(1)}, u32[]{:S(2)}, u32[]{:S(2)}) collective-permute-start(f32[128,256]{1,0:T(8,128)S(1)} %get-tuple-element.23.mine), channel_id=1, source_target_pairs={{0,8},{2,10},{4,12},{6,14},{8,0},{10,2},{12,4},{14,6},{16,24},{18,... | collective-permute-start | bytes 393224 | tf_op jit(solution)/shard_map/ppermute | solution.py:283
  12.9 4.8 %collective-permute-start.3 = (f32[8,256]{1,0:T(8,128)S(1)}, f32[8,256]{1,0:T(8,128)S(1)}, u32[]{:S(2)}, u32[]{:S(2)}) collective-permute-start(f32[8,256]{1,0:T(8,128)S(1)} %get-tuple-element.24), channel_id=1, source_target_pairs={{0,1},{1,0},{2,3},{3,2},{4,5},{5,4},{6,7},{7,6},{8,9},{9,8},{10,11... | collective-permute-start | bytes 24584 | tf_op jit(solution)/shard_map/ppermute | solution.py:311
  17.7 2.1 %collective-permute-start.4 = (f32[8,256]{1,0:T(8,128)S(1)}, f32[8,256]{1,0:T(8,128)S(1)}, u32[]{:S(2)}, u32[]{:S(2)}) collective-permute-start(f32[8,256]{1,0:T(8,128)S(1)} %get-tuple-element.24), channel_id=1, source_target_pairs={{0,3},{1,2},{2,1},{3,0},{4,7},{5,6},{6,5},{7,4},{8,11},{9,10},{10,... | collective-permute-start | bytes 24584 | tf_op jit(solution)/shard_map/ppermute | solution.py:313
  19.8 0.4 collective-permute-done.3.same
  20.2 4.4 %collective-permute-done.4.cross = f32[8,256]{1,0:T(8,128)S(1)} collective-permute-done((f32[8,256]{1,0:T(8,128)S(1)}, f32[8,256]{1,0:T(8,128)S(1)}, u32[]{:S(2)}, u32[]{:S(2)}) %collective-permute-start.4) | collective-permute-done | bytes 8224 | tf_op jit(solution)/shard_map/ppermute | solution.py:313
  24.7 0.6 shard_map.58
  25.3 1.1 %collective-permute-start.5 = (f32[8,256]{1,0:T(8,128)S(1)}, f32[8,256]{1,0:T(8,128)S(1)}, u32[]{:S(2)}, u32[]{:S(2)}) collective-permute-start(f32[8,256]{1,0:T(8,128)S(1)} %get-tuple-element.25.mine), channel_id=1, source_target_pairs={{0,4},{2,6},{4,0},{6,2},{8,12},{10,14},{12,8},{14,10},{16,20},{18,... | collective-permute-start | bytes 24584 | tf_op jit(solution)/shard_map/ppermute | solution.py:283
  26.4 1.4 %collective-permute-done.5.theirs.c_mate = f32[8,256]{1,0:T(8,128)S(1)} collective-permute-done((f32[8,256]{1,0:T(8,128)S(1)}, f32[8,256]{1,0:T(8,128)S(1)}, u32[]{:S(2)}, u32[]{:S(2)}) %collective-permute-start.5) | collective-permute-done | bytes 8224 | tf_op jit(solution)/shard_map/ppermute | solution.py:283
  27.9 1.6 %collective-permute-start.6 = (f32[8,256]{1,0:T(8,128)S(1)}, f32[8,256]{1,0:T(8,128)S(1)}, u32[]{:S(2)}, u32[]{:S(2)}) collective-permute-start(f32[8,256]{1,0:T(8,128)S(1)} %shard_map.59.c_mine), channel_id=1, source_target_pairs={{0,8},{2,10},{4,12},{6,14},{8,0},{10,2},{12,4},{14,6},{16,24},{18,... | collective-permute-start | bytes 24584 | tf_op jit(solution)/shard_map/ppermute | solution.py:283
  29.5 1.8 %collective-permute-done.6.c_theirs = f32[8,256]{1,0:T(8,128)S(1)} collective-permute-done((f32[8,256]{1,0:T(8,128)S(1)}, f32[8,256]{1,0:T(8,128)S(1)}, u32[]{:S(2)}, u32[]{:S(2)}) %collective-permute-start.6) | collective-permute-done | bytes 8224 | tf_op jit(solution)/shard_map/ppermute | solution.py:283
  31.3 0.4 shard_map.60
  31.7 1.3 %collective-permute-start.7 = (f32[136,256]{1,0:T(8,128)S(1)}, f32[136,256]{1,0:T(8,128)S(1)}, u32[]{:S(2)}, u32[]{:S(2)}) collective-permute-start(f32[136,256]{1,0:T(8,128)S(1)} %get-tuple-element.27.r0), channel_id=1, source_target_pairs={{0,16},{2,18},{4,20},{6,22},{8,24},{10,26},{12,28},{14,30},{16,0},... | collective-permute-start | bytes 417800 | tf_op jit(solution)/shard_map/ppermute | solution.py:283
  33.0 2.5 %collective-permute-start.8 = (f32[136,256]{1,0:T(8,128)S(1)}, f32[136,256]{1,0:T(8,128)S(1)}, u32[]{:S(2)}, u32[]{:S(2)}) collective-permute-start(f32[136,256]{1,0:T(8,128)S(1)} %get-tuple-element.27.r0), channel_id=1, source_target_pairs={{0,32},{2,34},{4,36},{6,38},{8,40},{10,42},{12,44},{14,46},{16,48}... | collective-permute-start | bytes 417800 | tf_op jit(solution)/shard_map/ppermute | solution.py:283
  35.5 0.2 collective-permute-start.9
  35.7 3.7 %collective-permute-done.8.r2 = f32[136,256]{1,0:T(8,128)S(1)} collective-permute-done((f32[136,256]{1,0:T(8,128)S(1)}, f32[136,256]{1,0:T(8,128)S(1)}, u32[]{:S(2)}, u32[]{:S(2)}) %collective-permute-start.8) | collective-permute-done | bytes 139296 | tf_op jit(solution)/shard_map/ppermute | solution.py:283
  39.4 1.5 %collective-permute-done.9.r3 = f32[136,256]{1,0:T(8,128)S(1)} collective-permute-done((f32[136,256]{1,0:T(8,128)S(1)}, f32[136,256]{1,0:T(8,128)S(1)}, u32[]{:S(2)}, u32[]{:S(2)}) %collective-permute-start.9) | collective-permute-done | bytes 139296 | tf_op jit(solution)/shard_map/ppermute | solution.py:283
  40.9 0.7 shard_map.61
  41.5 1.4 %collective-permute-start.10 = (f32[136,256]{1,0:T(8,128)S(1)}, f32[136,256]{1,0:T(8,128)S(1)}, u32[]{:S(2)}, u32[]{:S(2)}) collective-permute-start(f32[136,256]{1,0:T(8,128)S(1)} %get-tuple-element.28.r0), channel_id=1, source_target_pairs={{0,64},{2,66},{4,68},{6,70},{8,72},{10,74},{12,76},{14,78},{16,80}... | collective-permute-start | bytes 417800 | tf_op jit(solution)/shard_map/ppermute | solution.py:283
  42.9 2.6 %collective-permute-start.11 = (f32[136,256]{1,0:T(8,128)S(1)}, f32[136,256]{1,0:T(8,128)S(1)}, u32[]{:S(2)}, u32[]{:S(2)}) collective-permute-start(f32[136,256]{1,0:T(8,128)S(1)} %get-tuple-element.28.r0), channel_id=1, source_target_pairs={{0,128},{2,130},{4,132},{6,134},{8,136},{10,138},{12,140},{14,142}... | collective-permute-start | bytes 417800 | tf_op jit(solution)/shard_map/ppermute | solution.py:283
  45.5 0.3 collective-permute-done.10.r1
  45.8 3.7 %collective-permute-done.11.r2 = f32[136,256]{1,0:T(8,128)S(1)} collective-permute-done((f32[136,256]{1,0:T(8,128)S(1)}, f32[136,256]{1,0:T(8,128)S(1)}, u32[]{:S(2)}, u32[]{:S(2)}) %collective-permute-start.11) | collective-permute-done | bytes 139296 | tf_op jit(solution)/shard_map/ppermute | solution.py:283
  49.5 1.5 %collective-permute-done.12.r3 = f32[136,256]{1,0:T(8,128)S(1)} collective-permute-done((f32[136,256]{1,0:T(8,128)S(1)}, f32[136,256]{1,0:T(8,128)S(1)}, u32[]{:S(2)}, u32[]{:S(2)}) %collective-permute-start.12) | collective-permute-done | bytes 139296 | tf_op jit(solution)/shard_map/ppermute | solution.py:283
  51.0 1.4 %shard_map.62 = f32[40,256]{1,0:T(8,128)S(1)} custom-call(f32[136,256]{1,0:T(8,128)S(1)} %get-tuple-element.28.r0, f32[136,256]{1,0:T(8,128)S(1)} %collective-permute-done.10.r1, f32[136,256]{1,0:T(8,128)S(1)} %collective-permute-done.11.r2, f32[136,256]{1,0:T(8,128)S(1)} %collective-permute-done.12.r3, f32[136,256]{1,0:T(8,128)S(1)} %get-tuple-element.29.pz, ...), custom_call_target="tpu_custom_call" | custom-call | flops 200000000 | bytes 1000000 | tf_op jit(solution)/shard_map/pallas_call | solution.py:270
  52.4 6.9 %collective-permute-start.13 = (f32[40,256]{1,0:T(8,128)S(1)}, f32[40,256]{1,0:T(8,128)S(1)}, u32[]{:S(2)}, u32[]{:S(2)}) collective-permute-start(f32[40,256]{1,0:T(8,128)S(1)} %shard_map.62), channel_id=1, source_target_pairs={{0,2},{2,0},{4,6},{6,4},{8,10},{10,8},{12,14},{14,12},{16,18},{18,... | collective-permute-start | bytes 122888 | tf_op jit(solution)/shard_map/ppermute | solution.py:283
  59.3 0.9 %collective-permute-done.13.d = f32[40,256]{1,0:T(8,128)S(1)} collective-permute-done((f32[40,256]{1,0:T(8,128)S(1)}, f32[40,256]{1,0:T(8,128)S(1)}, u32[]{:S(2)}, u32[]{:S(2)}) %collective-permute-start.13) | collective-permute-done | bytes 40992 | tf_op jit(solution)/shard_map/ppermute | solution.py:283
  60.2 0.7 collective-permute-start.14
  60.9 1.8 %collective-permute-done.14.theirs.c_mate = f32[8,256]{1,0:T(8,128)S(1)} collective-permute-done((f32[8,256]{1,0:T(8,128)S(1)}, f32[8,256]{1,0:T(8,128)S(1)}, u32[]{:S(2)}, u32[]{:S(2)}) %collective-permute-start.14) | collective-permute-done | bytes 8224 | tf_op jit(solution)/shard_map/ppermute | solution.py:283
  62.8 1.2 %collective-permute-start.15 = (f32[8,256]{1,0:T(8,128)S(1)}, f32[8,256]{1,0:T(8,128)S(1)}, u32[]{:S(2)}, u32[]{:S(2)}) collective-permute-start(f32[8,256]{1,0:T(8,128)S(1)} %shard_map.63.mine), channel_id=1, source_target_pairs={{0,8},{2,10},{4,12},{6,14},{8,0},{10,2},{12,4},{14,6},{16,24},{18,... | collective-permute-start | bytes 24584 | tf_op jit(solution)/shard_map/ppermute | solution.py:283
  64.0 2.2 %collective-permute-done.15.theirs = f32[8,256]{1,0:T(8,128)S(1)} collective-permute-done((f32[8,256]{1,0:T(8,128)S(1)}, f32[8,256]{1,0:T(8,128)S(1)}, u32[]{:S(2)}, u32[]{:S(2)}) %collective-permute-start.15) | collective-permute-done | bytes 8224 | tf_op jit(solution)/shard_map/ppermute | solution.py:283
  66.5 2.0 %collective-permute-start.17 = (f32[8,256]{1,0:T(8,128)S(1)}, f32[8,256]{1,0:T(8,128)S(1)}, u32[]{:S(2)}, u32[]{:S(2)}) collective-permute-start(f32[8,256]{1,0:T(8,128)S(1)} %get-tuple-element.33.r0), channel_id=1, source_target_pairs={{0,32},{2,34},{4,36},{6,38},{8,40},{10,42},{12,44},{14,46},{16,48}... | collective-permute-start | bytes 24584 | tf_op jit(solution)/shard_map/ppermute | solution.py:283
  68.6 1.8 %collective-permute-start.18 = (f32[8,256]{1,0:T(8,128)S(1)}, f32[8,256]{1,0:T(8,128)S(1)}, u32[]{:S(2)}, u32[]{:S(2)}) collective-permute-start(f32[8,256]{1,0:T(8,128)S(1)} %get-tuple-element.33.r0), channel_id=1, source_target_pairs={{0,48},{2,50},{4,52},{6,54},{8,56},{10,58},{12,60},{14,62},{16,32}... | collective-permute-start | bytes 24584 | tf_op jit(solution)/shard_map/ppermute | solution.py:283
  70.4 0.4 collective-permute-done.17.r2
  70.8 1.5 %collective-permute-done.18.r3 = f32[8,256]{1,0:T(8,128)S(1)} collective-permute-done((f32[8,256]{1,0:T(8,128)S(1)}, f32[8,256]{1,0:T(8,128)S(1)}, u32[]{:S(2)}, u32[]{:S(2)}) %collective-permute-start.18) | collective-permute-done | bytes 8224 | tf_op jit(solution)/shard_map/ppermute | solution.py:283
  72.3 0.4 shard_map.65
  72.7 2.0 %collective-permute-start.20 = (f32[8,256]{1,0:T(8,128)S(1)}, f32[8,256]{1,0:T(8,128)S(1)}, u32[]{:S(2)}, u32[]{:S(2)}) collective-permute-start(f32[8,256]{1,0:T(8,128)S(1)} %get-tuple-element.36.e0), channel_id=1, source_target_pairs={{0,128},{2,130},{4,132},{6,134},{8,136},{10,138},{12,140},{14,142}... | collective-permute-start | bytes 24584 | tf_op jit(solution)/shard_map/ppermute | solution.py:283
  74.6 1.9 %collective-permute-start.21 = (f32[8,256]{1,0:T(8,128)S(1)}, f32[8,256]{1,0:T(8,128)S(1)}, u32[]{:S(2)}, u32[]{:S(2)}) collective-permute-start(f32[8,256]{1,0:T(8,128)S(1)} %get-tuple-element.36.e0), channel_id=1, source_target_pairs={{0,192},{2,194},{4,196},{6,198},{8,200},{10,202},{12,204},{14,206}... | collective-permute-start | bytes 24584 | tf_op jit(solution)/shard_map/ppermute | solution.py:283
  76.5 0.2 collective-permute-done.20.e2
  76.8 1.6 %collective-permute-done.21.e3 = f32[8,256]{1,0:T(8,128)S(1)} collective-permute-done((f32[8,256]{1,0:T(8,128)S(1)}, f32[8,256]{1,0:T(8,128)S(1)}, u32[]{:S(2)}, u32[]{:S(2)}) %collective-permute-start.21) | collective-permute-done | bytes 8224 | tf_op jit(solution)/shard_map/ppermute | solution.py:283
  78.3 1.1 %shard_map.66 = f32[4,128]{1,0:T(4,128)S(1)} custom-call(f32[8,256]{1,0:T(8,128)S(1)} %get-tuple-element.36.e0, f32[8,256]{1,0:T(8,128)S(1)} %collective-permute-done.19.e1, f32[8,256]{1,0:T(8,128)S(1)} %collective-permute-done.20.e2, f32[8,256]{1,0:T(8,128)S(1)} %collective-permute-done.21.e3, f32[136,256]{1,0:T(8,128)S(1)} %get-tuple-element.28.r0, ...), custom_call_target="tpu_custom_call" | custom-call | flops 200000000 | bytes 1000000 | tf_op jit(solution)/shard_map/pallas_call | solution.py:270
  79.5 6.2 %collective-permute-start.22 = (f32[2,128]{1,0:T(2,128)S(1)}, f32[2,128]{1,0:T(2,128)S(1)}, u32[]{:S(2)}, u32[]{:S(2)}) collective-permute-start(f32[2,128]{1,0:T(2,128)S(1)} %slice.10), channel_id=1, source_target_pairs={{0,2},{2,0},{4,6},{6,4},{8,10},{10,8},{12,14},{14,12},{16,18},{18,... | collective-permute-start | bytes 3080 | tf_op jit(solution)/shard_map/ppermute | solution.py:283
  85.6 0.8 collective-permute-done.22
  86.4 0.6 slice_select_fusion
  (13 shorter events, 0.7 us)
Async XLA Ops:
  1.1 4.5 %collective-permute-start = (f32[2,152,256]{2,1,0:T(8,128)S(1)}, f32[2,152,256]{2,1,0:T(8,128)S(1)}, u32[]{:S(2)}, u32[]{:S(2)}) collective-permute-start(f32[2,152,256]{2,1,0:T(8,128)S(1)} %get-tuple-element.22.own), channel_id=1, source_target_pairs={{0,2},{2,0},{4,6},{6,4},{8,10},{10,8},{12,14},{14,12},{16,18},{18,... | collective-permute-start | bytes 933896 | tf_op jit(solution)/shard_map/ppermute | solution.py:283
  6.2 4.8 %collective-permute-start.1 = (f32[128,256]{1,0:T(8,128)S(1)}, f32[128,256]{1,0:T(8,128)S(1)}, u32[]{:S(2)}, u32[]{:S(2)}) collective-permute-start(f32[128,256]{1,0:T(8,128)S(1)} %shard_map.56.mine), channel_id=1, source_target_pairs={{0,4},{2,6},{4,0},{6,2},{8,12},{10,14},{12,8},{14,10},{16,20},{18,... | collective-permute-start | bytes 393224 | tf_op jit(solution)/shard_map/ppermute | solution.py:283
  11.2 20.1 %collective-permute-start.2 = (f32[128,256]{1,0:T(8,128)S(1)}, f32[128,256]{1,0:T(8,128)S(1)}, u32[]{:S(2)}, u32[]{:S(2)}) collective-permute-start(f32[128,256]{1,0:T(8,128)S(1)} %get-tuple-element.23.mine), channel_id=1, source_target_pairs={{0,8},{2,10},{4,12},{6,14},{8,0},{10,2},{12,4},{14,6},{16,24},{18,... | collective-permute-start | bytes 393224 | tf_op jit(solution)/shard_map/ppermute | solution.py:283
  12.9 7.3 %collective-permute-start.3 = (f32[8,256]{1,0:T(8,128)S(1)}, f32[8,256]{1,0:T(8,128)S(1)}, u32[]{:S(2)}, u32[]{:S(2)}) collective-permute-start(f32[8,256]{1,0:T(8,128)S(1)} %get-tuple-element.24), channel_id=1, source_target_pairs={{0,1},{1,0},{2,3},{3,2},{4,5},{5,4},{6,7},{7,6},{8,9},{9,8},{10,11... | collective-permute-start | bytes 24584 | tf_op jit(solution)/shard_map/ppermute | solution.py:311
  17.7 7.0 %collective-permute-start.4 = (f32[8,256]{1,0:T(8,128)S(1)}, f32[8,256]{1,0:T(8,128)S(1)}, u32[]{:S(2)}, u32[]{:S(2)}) collective-permute-start(f32[8,256]{1,0:T(8,128)S(1)} %get-tuple-element.24), channel_id=1, source_target_pairs={{0,3},{1,2},{2,1},{3,0},{4,7},{5,6},{6,5},{7,4},{8,11},{9,10},{10,... | collective-permute-start | bytes 24584 | tf_op jit(solution)/shard_map/ppermute | solution.py:313
  25.3 2.5 %collective-permute-start.5 = (f32[8,256]{1,0:T(8,128)S(1)}, f32[8,256]{1,0:T(8,128)S(1)}, u32[]{:S(2)}, u32[]{:S(2)}) collective-permute-start(f32[8,256]{1,0:T(8,128)S(1)} %get-tuple-element.25.mine), channel_id=1, source_target_pairs={{0,4},{2,6},{4,0},{6,2},{8,12},{10,14},{12,8},{14,10},{16,20},{18,... | collective-permute-start | bytes 24584 | tf_op jit(solution)/shard_map/ppermute | solution.py:283
  27.9 3.4 %collective-permute-start.6 = (f32[8,256]{1,0:T(8,128)S(1)}, f32[8,256]{1,0:T(8,128)S(1)}, u32[]{:S(2)}, u32[]{:S(2)}) collective-permute-start(f32[8,256]{1,0:T(8,128)S(1)} %shard_map.59.c_mine), channel_id=1, source_target_pairs={{0,8},{2,10},{4,12},{6,14},{8,0},{10,2},{12,4},{14,6},{16,24},{18,... | collective-permute-start | bytes 24584 | tf_op jit(solution)/shard_map/ppermute | solution.py:283
  31.7 4.0 %collective-permute-start.7 = (f32[136,256]{1,0:T(8,128)S(1)}, f32[136,256]{1,0:T(8,128)S(1)}, u32[]{:S(2)}, u32[]{:S(2)}) collective-permute-start(f32[136,256]{1,0:T(8,128)S(1)} %get-tuple-element.27.r0), channel_id=1, source_target_pairs={{0,16},{2,18},{4,20},{6,22},{8,24},{10,26},{12,28},{14,30},{16,0},... | collective-permute-start | bytes 417800 | tf_op jit(solution)/shard_map/ppermute | solution.py:283
  33.0 6.4 %collective-permute-start.8 = (f32[136,256]{1,0:T(8,128)S(1)}, f32[136,256]{1,0:T(8,128)S(1)}, u32[]{:S(2)}, u32[]{:S(2)}) collective-permute-start(f32[136,256]{1,0:T(8,128)S(1)} %get-tuple-element.27.r0), channel_id=1, source_target_pairs={{0,32},{2,34},{4,36},{6,38},{8,40},{10,42},{12,44},{14,46},{16,48}... | collective-permute-start | bytes 417800 | tf_op jit(solution)/shard_map/ppermute | solution.py:283
  35.5 5.4 %collective-permute-start.9 = (f32[136,256]{1,0:T(8,128)S(1)}, f32[136,256]{1,0:T(8,128)S(1)}, u32[]{:S(2)}, u32[]{:S(2)}) collective-permute-start(f32[136,256]{1,0:T(8,128)S(1)} %get-tuple-element.27.r0), channel_id=1, source_target_pairs={{0,48},{2,50},{4,52},{6,54},{8,56},{10,58},{12,60},{14,62},{16,32}... | collective-permute-start | bytes 417800 | tf_op jit(solution)/shard_map/ppermute | solution.py:283
  41.5 4.3 %collective-permute-start.10 = (f32[136,256]{1,0:T(8,128)S(1)}, f32[136,256]{1,0:T(8,128)S(1)}, u32[]{:S(2)}, u32[]{:S(2)}) collective-permute-start(f32[136,256]{1,0:T(8,128)S(1)} %get-tuple-element.28.r0), channel_id=1, source_target_pairs={{0,64},{2,66},{4,68},{6,70},{8,72},{10,74},{12,76},{14,78},{16,80}... | collective-permute-start | bytes 417800 | tf_op jit(solution)/shard_map/ppermute | solution.py:283
  42.9 6.6 %collective-permute-start.11 = (f32[136,256]{1,0:T(8,128)S(1)}, f32[136,256]{1,0:T(8,128)S(1)}, u32[]{:S(2)}, u32[]{:S(2)}) collective-permute-start(f32[136,256]{1,0:T(8,128)S(1)} %get-tuple-element.28.r0), channel_id=1, source_target_pairs={{0,128},{2,130},{4,132},{6,134},{8,136},{10,138},{12,140},{14,142}... | collective-permute-start | bytes 417800 | tf_op jit(solution)/shard_map/ppermute | solution.py:283
  45.5 5.4 %collective-permute-start.12 = (f32[136,256]{1,0:T(8,128)S(1)}, f32[136,256]{1,0:T(8,128)S(1)}, u32[]{:S(2)}, u32[]{:S(2)}) collective-permute-start(f32[136,256]{1,0:T(8,128)S(1)} %get-tuple-element.28.r0), channel_id=1, source_target_pairs={{0,192},{2,194},{4,196},{6,198},{8,200},{10,202},{12,204},{14,206}... | collective-permute-start | bytes 417800 | tf_op jit(solution)/shard_map/ppermute | solution.py:283
  52.4 7.8 %collective-permute-start.13 = (f32[40,256]{1,0:T(8,128)S(1)}, f32[40,256]{1,0:T(8,128)S(1)}, u32[]{:S(2)}, u32[]{:S(2)}) collective-permute-start(f32[40,256]{1,0:T(8,128)S(1)} %shard_map.62), channel_id=1, source_target_pairs={{0,2},{2,0},{4,6},{6,4},{8,10},{10,8},{12,14},{14,12},{16,18},{18,... | collective-permute-start | bytes 122888 | tf_op jit(solution)/shard_map/ppermute | solution.py:283
  60.2 2.5 %collective-permute-start.14 = (f32[8,256]{1,0:T(8,128)S(1)}, f32[8,256]{1,0:T(8,128)S(1)}, u32[]{:S(2)}, u32[]{:S(2)}) collective-permute-start(f32[8,256]{1,0:T(8,128)S(1)} %slice.12.mine), channel_id=1, source_target_pairs={{0,4},{2,6},{4,0},{6,2},{8,12},{10,14},{12,8},{14,10},{16,20},{18,... | collective-permute-start | bytes 24584 | tf_op jit(solution)/shard_map/ppermute | solution.py:283
  62.8 3.4 %collective-permute-start.15 = (f32[8,256]{1,0:T(8,128)S(1)}, f32[8,256]{1,0:T(8,128)S(1)}, u32[]{:S(2)}, u32[]{:S(2)}) collective-permute-start(f32[8,256]{1,0:T(8,128)S(1)} %shard_map.63.mine), channel_id=1, source_target_pairs={{0,8},{2,10},{4,12},{6,14},{8,0},{10,2},{12,4},{14,6},{16,24},{18,... | collective-permute-start | bytes 24584 | tf_op jit(solution)/shard_map/ppermute | solution.py:283
  66.4 3.9 %collective-permute-start.16 = (f32[8,256]{1,0:T(8,128)S(1)}, f32[8,256]{1,0:T(8,128)S(1)}, u32[]{:S(2)}, u32[]{:S(2)}) collective-permute-start(f32[8,256]{1,0:T(8,128)S(1)} %get-tuple-element.33.r0), channel_id=1, source_target_pairs={{0,16},{2,18},{4,20},{6,22},{8,24},{10,26},{12,28},{14,30},{16,0},... | collective-permute-start | bytes 24584 | tf_op jit(solution)/shard_map/ppermute | solution.py:283
  66.5 4.3 %collective-permute-start.17 = (f32[8,256]{1,0:T(8,128)S(1)}, f32[8,256]{1,0:T(8,128)S(1)}, u32[]{:S(2)}, u32[]{:S(2)}) collective-permute-start(f32[8,256]{1,0:T(8,128)S(1)} %get-tuple-element.33.r0), channel_id=1, source_target_pairs={{0,32},{2,34},{4,36},{6,38},{8,40},{10,42},{12,44},{14,46},{16,48}... | collective-permute-start | bytes 24584 | tf_op jit(solution)/shard_map/ppermute | solution.py:283
  68.6 3.7 %collective-permute-start.18 = (f32[8,256]{1,0:T(8,128)S(1)}, f32[8,256]{1,0:T(8,128)S(1)}, u32[]{:S(2)}, u32[]{:S(2)}) collective-permute-start(f32[8,256]{1,0:T(8,128)S(1)} %get-tuple-element.33.r0), channel_id=1, source_target_pairs={{0,48},{2,50},{4,52},{6,54},{8,56},{10,58},{12,60},{14,62},{16,32}... | collective-permute-start | bytes 24584 | tf_op jit(solution)/shard_map/ppermute | solution.py:283
  72.7 3.9 %collective-permute-start.19 = (f32[8,256]{1,0:T(8,128)S(1)}, f32[8,256]{1,0:T(8,128)S(1)}, u32[]{:S(2)}, u32[]{:S(2)}) collective-permute-start(f32[8,256]{1,0:T(8,128)S(1)} %get-tuple-element.36.e0), channel_id=1, source_target_pairs={{0,64},{2,66},{4,68},{6,70},{8,72},{10,74},{12,76},{14,78},{16,80}... | collective-permute-start | bytes 24584 | tf_op jit(solution)/shard_map/ppermute | solution.py:283
  72.7 4.1 %collective-permute-start.20 = (f32[8,256]{1,0:T(8,128)S(1)}, f32[8,256]{1,0:T(8,128)S(1)}, u32[]{:S(2)}, u32[]{:S(2)}) collective-permute-start(f32[8,256]{1,0:T(8,128)S(1)} %get-tuple-element.36.e0), channel_id=1, source_target_pairs={{0,128},{2,130},{4,132},{6,134},{8,136},{10,138},{12,140},{14,142}... | collective-permute-start | bytes 24584 | tf_op jit(solution)/shard_map/ppermute | solution.py:283
  74.6 3.7 %collective-permute-start.21 = (f32[8,256]{1,0:T(8,128)S(1)}, f32[8,256]{1,0:T(8,128)S(1)}, u32[]{:S(2)}, u32[]{:S(2)}) collective-permute-start(f32[8,256]{1,0:T(8,128)S(1)} %get-tuple-element.36.e0), channel_id=1, source_target_pairs={{0,192},{2,194},{4,196},{6,198},{8,200},{10,202},{12,204},{14,206}... | collective-permute-start | bytes 24584 | tf_op jit(solution)/shard_map/ppermute | solution.py:283
  79.5 7.0 %collective-permute-start.22 = (f32[2,128]{1,0:T(2,128)S(1)}, f32[2,128]{1,0:T(2,128)S(1)}, u32[]{:S(2)}, u32[]{:S(2)}) collective-permute-start(f32[2,128]{1,0:T(2,128)S(1)} %slice.10), channel_id=1, source_target_pairs={{0,2},{2,0},{4,6},{6,4},{8,10},{10,8},{12,14},{14,12},{16,18},{18,... | collective-permute-start | bytes 3080 | tf_op jit(solution)/shard_map/ppermute | solution.py:283
